TPU v7x, 32 devices: a whole 2x2x4 slice. The times are simulated.
32 devices in a mesh: seq: 8 (over z, x), dp: 4 (over y, core).
Axes of the slice: x: 2, y: 2, z: 4, core: 2. Of those that a mesh axis runs over, the one named last changes fastest.
Arguments:
- inputs: bfloat16 [4, 1024, 8192], P('dp', 'seq'), may hold values from -8 to 8
- adapter_down_weight: bfloat16 [8192, 128], replicated, may hold values from -0.0625 to 0.0625
- adapter_up_weight: bfloat16 [384, 128], replicated, may hold values from -0.3125 to 0.3125
- query: bfloat16 [4, 1024, 128], P('dp', 'seq'), may hold values from -6 to 6
- key: bfloat16 [4, 1024, 128], P('dp', 'seq'), may hold values from -6 to 6
- value: bfloat16 [4, 1024, 128], P('dp', 'seq'), may hold values from -6 to 6
- output_gradient: bfloat16 [4, 1024, 128], P('dp', 'seq'), may hold values from -6 to 6
Outputs:
- query_grad: bfloat16 [4, 1024, 128], P('dp', 'seq')
- key_grad: bfloat16 [4, 1024, 128], P('dp', 'seq')
- value_grad: bfloat16 [4, 1024, 128], P('dp', 'seq')
- down_grad: float32 [8192, 128], P('dp')
- up_grad: float32 [384, 128], P('dp')
All inputs are finite; a program needn't handle non-finite values.
Results may differ from a plain program's by a relative error of at most 0.0058.
Values sent between devices are 32-bit elements; how exact they have to be, the bound alone decides.
A program may use at most 64 MiB of HBM per device.

v0:
```python
import functools
import math

import jax
import jax.numpy as jnp
from jax import lax
from jax.experimental import pallas as pl
from jax.experimental.pallas import tpu as pltpu
from jax.sharding import PartitionSpec as P

HEAD_SIZE = 128
LOCAL_HEADS = 1


def entering(part, axis, combine, identity, reverse):
    count = lax.axis_size(axis)
    place = lax.axis_index(axis)
    ahead = count - 1 - place if reverse else place
    gathered = lax.all_gather(part, axis)
    state = jnp.zeros_like(part) + jnp.asarray(identity, part.dtype)

    def one(turn, state):
        source = count - 1 - turn if reverse else turn
        return combine(state, lax.dynamic_index_in_dim(gathered, source, 0, False))

    return lax.fori_loop(0, ahead, one, state)


def add_states(earlier, later):
    return earlier + later


def rounded_values(array):
    return array.astype(jnp.bfloat16)


def local(inputs, adapter_down_weight, adapter_up_weight, query, key, value, output_gradient):
    rows = query.shape[1]
    width = query.shape[2]
    seq_count = lax.axis_size("seq")
    dp_count = lax.axis_size("dp")
    length = rows * seq_count
    factor = 1.0 / math.sqrt(HEAD_SIZE * length)
    queries = query.reshape(rows, LOCAL_HEADS, HEAD_SIZE)
    keys = key.reshape(rows, LOCAL_HEADS, HEAD_SIZE)
    values = value.reshape(rows, LOCAL_HEADS, HEAD_SIZE)
    grads_out = output_gradient.reshape(rows, LOCAL_HEADS, HEAD_SIZE)
    kv_state = jnp.einsum("thi,thj->hij", keys, values, preferred_element_type=jnp.float32)
    qg_state = jnp.einsum("thi,thj->hij", queries, grads_out, preferred_element_type=jnp.float32)
    zeros = jnp.zeros_like(kv_state)
    prefix = entering(kv_state, "seq", add_states, zeros, False)
    suffix = entering(qg_state, "seq", add_states, zeros, True)
    prefix = rounded_values(prefix)
    suffix = rounded_values(suffix)
    rows_idx = lax.broadcasted_iota(jnp.int32, (rows, rows), 0)
    cols_idx = lax.broadcasted_iota(jnp.int32, (rows, rows), 1)
    causal = rows_idx >= cols_idx
    grad_scores = rounded_values(
        jnp.where(
            causal,
            jnp.einsum("thj,shj->hts", grads_out, values, preferred_element_type=jnp.float32),
            0.0,
        )
    )
    scores = rounded_values(
        jnp.where(
            causal,
            jnp.einsum("thi,shi->hts", queries, keys, preferred_element_type=jnp.float32),
            0.0,
        )
    )
    query_grad = jnp.einsum(
        "hts,shi->thi", grad_scores, keys, preferred_element_type=jnp.float32
    ) + jnp.einsum("thj,hij->thi", grads_out, prefix, preferred_element_type=jnp.float32)
    key_grad = jnp.einsum(
        "hts,thi->shi", grad_scores, queries, preferred_element_type=jnp.float32
    ) + jnp.einsum("shj,hij->shi", values, suffix, preferred_element_type=jnp.float32)
    value_grad = jnp.einsum(
        "hts,thj->shj", scores, grads_out, preferred_element_type=jnp.float32
    ) + jnp.einsum("shi,hij->shj", keys, suffix, preferred_element_type=jnp.float32)
    query_grad = rounded_values(factor * query_grad).reshape(rows, width)
    key_grad = rounded_values(factor * key_grad).reshape(rows, width)
    value_grad = rounded_values(factor * value_grad).reshape(rows, width)
    flattened = inputs.reshape(rows, inputs.shape[2])
    gradient_list = jnp.concatenate([query_grad, key_grad, value_grad], axis=1)
    low_rank_state = rounded_values(
        jnp.dot(flattened, adapter_down_weight, preferred_element_type=jnp.float32)
    )
    low_rank_gradient = rounded_values(
        jnp.dot(gradient_list, adapter_up_weight, preferred_element_type=jnp.float32)
    )
    inverse = 1.0 / math.sqrt(length * dp_count)
    contract = (((0,), (0,)), ((), ()))
    down_part = lax.psum_scatter(
        lax.dot_general(flattened, low_rank_gradient, contract, preferred_element_type=jnp.float32)
        * inverse,
        "dp",
        scatter_dimension=0,
        tiled=True,
    )
    up_term = (
        lax.dot_general(gradient_list, low_rank_state, contract, preferred_element_type=jnp.float32)
        * inverse
    )
    up_part = lax.psum_scatter(up_term, "dp", scatter_dimension=0, tiled=True)
    down_grad, up_grad = lax.psum((down_part, up_part), "seq")
    return (
        query_grad.reshape(1, rows, width),
        key_grad.reshape(1, rows, width),
        value_grad.reshape(1, rows, width),
        down_grad,
        up_grad,
    )


MESH = pl.DeviceIdType.MESH
CORES = 2
CHUNKS = 16
SKEW = 3


def fits(seq_count, dp_count):
    depth = seq_count // 2
    return dp_count == 2 * CORES and depth >= 2 and seq_count % 2 == 0 and depth & (depth - 1) == 0


def dot(a, b, da, db):
    return lax.dot_general(a, b, (((da,), (db,)), ((), ())), preferred_element_type=jnp.float32)


def fused_kernel(
    depth, factor, inverse,
    x_hbm, w_hbm, u_ref, q_ref, k_ref, v_ref, g_ref,
    qo_ref, ko_ref, vo_ref, down_ref, up_ref,
    x_ref, w_ref, xs_ref, xr_ref, xt_ref,
    st_ref, pair_ref, kvr_ref, qgr_ref, ox_ref, sxs_ref, sxr_ref,
    ls_ref, lr_ref, ups_ref, upr_ref, fg_ref,
    ys_ref, yr_ref, acc_ref, xrs_ref, zs_ref, zr_ref, us_ref, ur_ref,
    load_sem, core_s, core_r, kv_s, kv_r, qg_s, qg_r, sx_s, sx_r,
    y_s, y_r, x_s, x_r, z_s, z_r, b_s, b_r,
):
    seq = lax.axis_index("seq")
    dp = lax.axis_index("dp")
    z, x = seq // 2, seq % 2
    y, c = dp // CORES, dp % CORES
    mate = {"seq": seq, "dp": y * CORES + (1 - c)}
    across = {"seq": seq, "dp": (1 - y) * CORES + c}
    beside = {"seq": z * 2 + (1 - x), "dp": dp}

    corner = {"seq": (z + 1 - 2 * (z % 2)) * 2 + (1 - x), "dp": dp}

    def along(other):
        return {"seq": other * 2 + x, "dp": dp}

    load_x = pltpu.make_async_copy(x_hbm, x_ref, load_sem.at[0])
    load_w = pltpu.make_async_copy(w_hbm, w_ref, load_sem.at[1])
    load_x.start()
    load_w.start()

    barrier = pltpu.get_barrier_semaphore()
    friends = [mate, across, beside, corner] + [along(lax.rem(z + d, depth)) for d in range(1, depth)]
    for friend in friends:
        pl.semaphore_signal(barrier, inc=1, device_id=friend, device_id_type=MESH)

    rows = q_ref.shape[0]
    shard = down_ref.shape[0]
    ushard = up_ref.shape[0]
    width = q_ref.shape[1]
    q, k, v, g = q_ref[...], k_ref[...], v_ref[...], g_ref[...]
    st_ref[0] = dot(k, v, 0, 0)
    st_ref[1] = dot(q, g, 0, 0)
    pl.semaphore_wait(barrier, len(friends))

    def remote(src, dst, ssem, rsem, where):
        return pltpu.make_async_remote_copy(
            src_ref=src, dst_ref=dst, send_sem=ssem, recv_sem=rsem, device_id=where, device_id_type=MESH
        )

    lead = width // 2
    first, second = slice(0, lead), slice(lead, width)
    other = remote(st_ref.at[:, second, :], ox_ref, sx_s.at[1], sx_r.at[1], beside)
    other.start()

    def scan(source, part, at):
        ups, downs = [], []
        for d in range(1, depth):
            slot = at * (depth - 1) + d - 1
            ups.append(remote(source.at[0, part, :], kvr_ref.at[d - 1, part, :], kv_s.at[slot], kv_r.at[slot], along(lax.rem(z + d, depth))))
            downs.append(remote(source.at[1, part, :], qgr_ref.at[d - 1, part, :], qg_s.at[slot], qg_r.at[slot], along(lax.rem(z - d + depth, depth))))
        for d in range(1, depth):
            pl.when(z + d < depth)(ups[d - 1].start)
            pl.when(z >= d)(downs[d - 1].start)
        return ups, downs

    def collect(ups, downs, part):
        sxs_ref[:, part, :] = jnp.zeros((2, lead, width), jnp.float32)
        for d in range(1, depth):
            @pl.when(z >= d)
            def _(d=d):
                ups[d - 1].wait_recv()
                sxs_ref[0, part, :] += kvr_ref[d - 1, part, :]

            @pl.when(z + d < depth)
            def _(d=d):
                downs[d - 1].wait_recv()
                sxs_ref[1, part, :] += qgr_ref[d - 1, part, :]

    scan_a = scan(st_ref, first, 0)

    load_x.wait()
    core_copies = []
    for part in range(2):
        cols = pl.ds(pl.multiple_of((part * CORES + 1 - c) * shard, 128), shard)
        xs_ref[part] = x_ref[:, cols].astype(jnp.float32)
        copy = remote(xs_ref.at[part], xr_ref.at[part], core_s.at[part], core_r.at[part], mate)
        copy.start()
        core_copies.append(copy)

    other.wait_recv()
    pair_ref[:, second, :] = st_ref[:, second, :] + ox_ref[...]
    scan_b = scan(pair_ref, second, 1)

    r_idx = lax.broadcasted_iota(jnp.int32, (rows, rows), 0)
    c_idx = lax.broadcasted_iota(jnp.int32, (rows, rows), 1)
    causal = r_idx >= c_idx
    gs = jnp.where(causal, dot(g, v, 1, 1), 0.0).astype(jnp.bfloat16)
    sc = jnp.where(causal, dot(q, k, 1, 1), 0.0).astype(jnp.bfloat16)
    q_in = dot(gs, k, 1, 0)
    k_in = dot(gs, q, 0, 0)
    v_in = dot(sc, g, 0, 0)

    for part in range(2):
        cols = pl.ds(pl.multiple_of((part * CORES + c) * shard, 128), shard)
        xt_ref[part, :, 0:rows] = x_ref[:, cols].T

    collect(*scan_a, first)
    lead_sum = sxs_ref[:, first, :]

    @pl.when(x == 0)
    def _():
        sxs_ref[0, first, :] += st_ref[0, first, :]

    @pl.when(x == 1)
    def _():
        sxs_ref[1, first, :] += st_ref[1, first, :]

    swap = remote(sxs_ref.at[:, first, :], sxr_ref, sx_s.at[0], sx_r.at[0], beside)
    swap.start()

    for part in range(2):
        core_copies[part].wait_recv()
        xt_ref[part, :, rows:] = xr_ref[part].astype(jnp.bfloat16).T

    collect(*scan_b, second)

    @pl.when(x == 1)
    def _():
        sxs_ref[0, second, :] += ox_ref[0]

    @pl.when(x == 0)
    def _():
        sxs_ref[1, second, :] += ox_ref[1]

    swap.wait_recv()
    states = jnp.concatenate([lead_sum + sxr_ref[...], sxs_ref[:, second, :]], axis=1).astype(jnp.bfloat16)
    prefix, suffix = states[0], states[1]
    q_grad = (factor * (q_in + dot(g, prefix, 1, 1))).astype(jnp.bfloat16)
    k_grad = (factor * (k_in + dot(v, suffix, 1, 1))).astype(jnp.bfloat16)
    v_grad = (factor * (v_in + dot(k, suffix, 1, 0))).astype(jnp.bfloat16)
    fg = jnp.concatenate([q_grad, k_grad, v_grad], axis=1)
    low_grad = dot(fg, u_ref[...], 1, 0).astype(jnp.bfloat16)
    ls_ref[...] = low_grad.astype(jnp.float32)
    low_copy = remote(ls_ref, lr_ref, core_s.at[2], core_r.at[2], mate)
    low_copy.start()
    qo_ref[...] = q_grad
    ko_ref[...] = k_grad
    vo_ref[...] = v_grad

    low_copy.wait_recv()
    both = jnp.concatenate([low_grad, lr_ref[...].astype(jnp.bfloat16)], axis=0)

    size = shard // CHUNKS
    pieces = [(i * size, size) for i in range(CHUNKS)] + [(shard, ushard)]
    count = len(pieces)

    def partial(i, part):
        off, n = pieces[i]
        if off < shard:
            return jnp.dot(xt_ref[part, off : off + n, :], both, preferred_element_type=jnp.float32)
        mine = pl.ds(pl.multiple_of((part * CORES + c) * ushard, 8), ushard)
        return fg_ref[mine, :] + upr_ref[part]

    def half(i, which):
        off, n = pieces[i]
        return pl.ds(pl.multiple_of(off + which * (n // 2), 8), n // 2)

    def place(i, which, cuts):
        off, n = pieces[i]
        ref, base = (down_ref, off) if off < shard else (up_ref, 0)
        return ref.at[pl.ds(pl.multiple_of(base + which * (n // cuts), 8), n // cuts), :]

    y_copies, x_copies = [], []
    b_copies = []
    top = depth.bit_length() - 1
    z_copies = [[] for _ in range(top)]
    b = z % 2

    def flip(level):
        bit = 1 << level
        return z + bit - 2 * bit * ((z // bit) % 2)

    def y_stage(i):
        off, n = pieces[i]
        ys_ref[off : off + n, :] = partial(i, 1 - y)
        copy = remote(ys_ref.at[off : off + n, :], yr_ref.at[off : off + n, :], y_s.at[i], y_r.at[i], across)
        copy.start()
        y_copies.append(copy)

    for i in range(count - 1):
        y_stage(i)
    load_w.wait()
    low = jnp.dot(x_ref[...], w_ref[...], preferred_element_type=jnp.float32).astype(jnp.bfloat16)
    up_all = dot(fg, low, 0, 0)
    fg_ref[...] = up_all
    for part in range(2):
        rng = pl.ds(pl.multiple_of((part * CORES + 1 - c) * ushard, 8), ushard)
        ups_ref[part] = fg_ref[rng, :]
    up_copy = remote(ups_ref, upr_ref, core_s.at[3], core_r.at[3], mate)
    up_copy.start()

    up_copy.wait_recv()
    y_stage(count - 1)

    def x_stage(i):
        off, n = pieces[i]
        own = partial(i, y)
        y_copies[i].wait_recv()
        acc_ref[off : off + n, :] = own + yr_ref[off : off + n, :]
        h = n // 2
        short = pl.ds(off // 2, h)
        copy = remote(acc_ref.at[half(i, 1 - x), :], xrs_ref.at[short, :], x_s.at[i], x_r.at[i], beside)
        copy.start()
        x_copies.append(copy)

    def z_stage(i, level):
        off, n = pieces[i]
        h, e = n // 2, n // 4
        if level == 0:
            x_copies[i].wait_recv()
            zs_ref[off // 2 : off // 2 + h, :] = acc_ref[half(i, x), :] + xrs_ref[off // 2 : off // 2 + h, :]
            away = pl.ds(pl.multiple_of(off // 2 + (1 - b) * e, 8), e)
            source, target = zs_ref.at[away, :], zr_ref.at[off // 4 : off // 4 + e, :]
        else:
            z_copies[level - 1][i].wait_recv()
            short = slice(off // 4, off // 4 + e)
            if level == 1:
                kept = zs_ref[pl.ds(pl.multiple_of(off // 2 + b * e, 8), e), :] + zr_ref[short, :]
            else:
                kept = us_ref[level - 2, short, :] + ur_ref[level - 2, short, :]
            if level == top:
                spot = place(i, x * 2 + b, 4)
                spot[...] = kept * inverse
                for at, where in enumerate((beside, along(flip(0)), corner)):
                    copy = remote(spot, place(i, x * 2 + b, 4), b_s.at[at, i], b_r.at[at, i], where)
                    copy.start()
                    b_copies.append(copy)
                return
            us_ref[level - 1, short, :] = kept
            source, target = us_ref.at[level - 1, short, :], ur_ref.at[level - 1, short, :]
        copy = remote(source, target, z_s.at[level, i], z_r.at[level, i], along(flip(level)))
        copy.start()
        z_copies[level].append(copy)

    levels = top + 1
    for t in range(count + levels * SKEW):
        if t < count:
            x_stage(t)
        for level in range(levels):
            i = t - SKEW * (1 + level)
            if 0 <= i < count:
                z_stage(i, level)

    for copy in b_copies:
        copy.wait_recv()
    for ups, downs in (scan_a, scan_b):
        for d in range(1, depth):
            pl.when(z + d < depth)(ups[d - 1].wait_send)
            pl.when(z >= d)(downs[d - 1].wait_send)
    for copy in core_copies + [other, swap, low_copy, up_copy] + y_copies + x_copies + sum(z_copies, []) + b_copies:
        copy.wait_send()


def write_out(*refs):
    copies = [pltpu.make_async_copy(refs[i], refs[5 + i], refs[10].at[i]) for i in range(5)]
    for copy in copies:
        copy.start()
    for copy in copies:
        copy.wait()


def fast(inputs, adapter_down_weight, adapter_up_weight, query, key, value, output_gradient):
    rows, width = query.shape[1:]
    model = inputs.shape[2]
    rank = adapter_down_weight.shape[1]
    features = adapter_up_weight.shape[0]
    seq_count = lax.axis_size("seq")
    dp_count = lax.axis_size("dp")
    length = rows * seq_count
    factor = 1.0 / math.sqrt(HEAD_SIZE * length)
    inverse = 1.0 / math.sqrt(length * dp_count)
    depth = seq_count // 2
    stages = depth.bit_length() - 1
    shard, ushard = model // dp_count, features // dp_count
    total = shard + ushard
    count = CHUNKS + 1
    f32, bf16 = jnp.float32, jnp.bfloat16
    dma = pltpu.SemaphoreType.DMA
    vmem = pl.BlockSpec(memory_space=pltpu.VMEM)
    hbm = pl.BlockSpec(memory_space=pl.ANY)
    shapes = [jax.ShapeDtypeStruct((rows, width), bf16)] * 3 + [
        jax.ShapeDtypeStruct((shard, rank), f32),
        jax.ShapeDtypeStruct((ushard, rank), f32),
    ]
    out = pl.pallas_call(
        functools.partial(fused_kernel, depth, factor, inverse),
        out_shape=shapes,
        in_specs=[hbm, hbm] + [vmem] * 5,
        out_specs=[vmem] * 5,
        scratch_shapes=[
            pltpu.VMEM((rows, model), bf16),
            pltpu.VMEM((model, rank), bf16),
            pltpu.VMEM((2, rows, shard), f32),
            pltpu.VMEM((2, rows, shard), f32),
            pltpu.VMEM((2, shard, 2 * rows), bf16),
            pltpu.VMEM((2, width, width), f32),
            pltpu.VMEM((2, width, width), f32),
            pltpu.VMEM((depth - 1, width, width), f32),
            pltpu.VMEM((depth - 1, width, width), f32),
            pltpu.VMEM((2, width // 2, width), f32),
            pltpu.VMEM((2, width, width), f32),
            pltpu.VMEM((2, width // 2, width), f32),
            pltpu.VMEM((rows, rank), f32),
            pltpu.VMEM((rows, rank), f32),
            pltpu.VMEM((2, ushard, rank), f32),
            pltpu.VMEM((2, ushard, rank), f32),
            pltpu.VMEM((features, rank), f32),
            pltpu.VMEM((total, rank), f32),
            pltpu.VMEM((total, rank), f32),
            pltpu.VMEM((total, rank), f32),
            pltpu.VMEM((total // 2, rank), f32),
            pltpu.VMEM((total // 2, rank), f32),
            pltpu.VMEM((total // 4, rank), f32),
            pltpu.VMEM((max(stages - 1, 1), total // 4, rank), f32),
            pltpu.VMEM((max(stages - 1, 1), total // 4, rank), f32),
            dma((2,)), dma((4,)), dma((4,)),
            dma((2 * depth - 2,)), dma((2 * depth - 2,)), dma((2 * depth - 2,)), dma((2 * depth - 2,)),
            dma((2,)), dma((2,)),
            dma((count,)), dma((count,)), dma((count,)), dma((count,)),
            dma((stages, count)), dma((stages, count)),
            dma((3, count)), dma((3, count)),
        ],
        compiler_params=pltpu.CompilerParams(
            collective_id=0, has_side_effects=True
        ),
    )(
        inputs.reshape(rows, model), adapter_down_weight, adapter_up_weight,
        query.reshape(rows, width), key.reshape(rows, width),
        value.reshape(rows, width), output_gradient.reshape(rows, width),
    )
    out = pl.pallas_call(
        write_out,
        out_shape=shapes,
        in_specs=[vmem] * 5,
        out_specs=[hbm] * 5,
        scratch_shapes=[dma((5,))],
    )(*out)
    return tuple(part.reshape(1, rows, width) for part in out[:3]) + tuple(out[3:])


def solution(mesh):
    fused = fits(mesh.shape["seq"], mesh.shape["dp"])
    chosen = fast if fused else local
    return jax.shard_map(
        chosen,
        mesh=mesh,
        in_specs=(
            P("dp", "seq", None),
            P(),
            P(),
            P("dp", "seq", None),
            P("dp", "seq", None),
            P("dp", "seq", None),
            P("dp", "seq", None),
        ),
        out_specs=(
            P("dp", "seq", None),
            P("dp", "seq", None),
            P("dp", "seq", None),
            P("dp", None),
            P("dp", None),
        ),
        check_vma=False,
    )
```

profile of v0, /device:TPU:0, one launch (start us, length us, event | category | flops | bytes accessed | tf_op | source)
XLA Modules:
  0.0 62.5 jit_solution(12820893498334411331)
XLA Ops:
  0.6 59.5 %shard_map.110 = (bf16[128,128]{1,0:T(8,128)(2,1)}, bf16[128,128]{1,0:T(8,128)(2,1)}, bf16[128,128]{1,0:T(8,128)(2,1)}, f32[2048,128]{1,0:T(8,128)}, f32[96,128]{1,0:T(8,128)}) custom-call(bf16[128,8192]{1,0:T(8,128)(2,1)} %bitcast.8, bf16[8192,128]{1,0:T(8,128)(2,1)} %w_hbm.1, bf16[384,128]{1,0:T(8,128)(2,1)} %u_ref.1, bf16[128,128]{1,0:T(8,128)(2,1)} %bitcast.9, ...), custom_call_target="tpu_custom_call" | custom-call | tf_op jit(solution)/shard_map/pallas_call | solution.py:424
  60.2 2.3 %shard_map.111 = (bf16[128,128]{1,0:T(8,128)(2,1)}, bf16[128,128]{1,0:T(8,128)(2,1)}, bf16[128,128]{1,0:T(8,128)(2,1)}, f32[2048,128]{1,0:T(8,128)}, f32[96,128]{1,0:T(8,128)}) custom-call(bf16[128,128]{1,0:T(8,128)(2,1)} %get-tuple-element.15.refs_0_, bf16[128,128]{1,0:T(8,128)(2,1)} %get-tuple-element.16.refs_1_, ...), custom_call_target="tpu_custom_call" | custom-call | tf_op jit(solution)/shard_map/pallas_call | solution.py:470
where the time goes:
time: 62.7 us; the launch traced here: 62.5 us
  Pallas kernels  61.8 us (99%)
  between operations  0.64 us (1%)
    pallas_call x1, Pallas kernels, fast(): pl.pallas_call(functools.partial(fused_kernel, depth, factor, inverse), o...  59.5 us
    pallas_call x1, Pallas kernels, fast(): pl.pallas_call(write_out, out_shape=shapes, in_specs=[vmem] * 5, out_spec...  2.3 us

commit v1 on v0

--- a/solution.py
+++ b/solution.py
@@ -115,13 +115,130 @@
 
 MESH = pl.DeviceIdType.MESH
 CORES = 2
-CHUNKS = 16
-SKEW = 3
+LINE = 4
+KINDS = 8
+Y, X, ZI, ZM, ZF, ZO, B, F = range(KINDS)
+ROLES = ("outer", "inner")
+PIECES = 16
+UP_AT = 8
+X_FIRST = (0, 1, 2, 3)
+RELAYED = (2, 2, 2, 2, 2, 2, 2, 1, 1, 1, 1, 1, 1, 0, 3, 3, 3)
+RATE, HOP, MORE = 92.0, 1.75, 0.75
+DEEP_Y, DEEP_X = 2.0, 1.0
+COST = {"y_send": 0.17, "x_send": 0.18, "x_first": 0.32}
+
+
+def cut(shard, ushard):
+    size = shard // PIECES
+    spans = [(i * size, size) for i in range(PIECES)]
+    spans.insert(UP_AT, (shard, ushard))
+    return [(off, n, i in X_FIRST, RELAYED[i]) for i, (off, n) in enumerate(spans)]
+
+
+def landing(pieces):
+    slots = {}
+    for i, (_, _, _, mode) in enumerate(pieces):
+        for kind in (Y, X, ZI, ZM):
+            slots[kind, i] = len(slots)
+        if mode in (0, 2):
+            slots[ZO, i] = slots[ZI, i]
+        if mode == 1:
+            slots[B, i] = len(slots)
+        if mode == 2:
+            slots[B, i] = slots[ZM, i]
+        if mode == 3:
+            slots[ZF, i] = len(slots)
+    return slots
+
+
+def plan(pieces):
+    free, links, arrive = {}, {}, {}
+    out = {role: [] for role in ROLES}
+    todo = {role: [] for role in ROLES}
+    starts = {role: {"y_send": [], "x_first": []} for role in ROLES}
+    for i, (_, _, first_x, mode) in enumerate(pieces):
+        landed = Y if first_x else X
+        for role in ROLES:
+            starts[role]["x_first" if first_x else "y_send"].append(i)
+            todo[role].append(("y_second", i, (X,)) if first_x else ("x_send", i, (Y,)))
+        todo["outer"].append(("z_in", i, (landed,)))
+        if mode == 3:
+            todo["inner"] += [("z_own", i, (landed,)), ("z_out", i, (ZI, ZM, ZF))]
+        else:
+            todo["inner"] += [("z_mid", i, (landed, ZI)), ("z_out", i, (ZM,))]
+        if mode in (0, 2):
+            todo["outer"].append(("relay", i, (ZO,)))
+        if mode in (1, 2):
+            todo["inner" if mode == 1 else "outer"].append(("forward", i, (B,)))
+
+    def move(role, link, rows, now, to, kind, i, then=None):
+        begin = max(now, links.get((role, link), 0.0))
+        done = begin + rows / RATE
+        links[role, link] = done
+        if then:
+            begin = max(begin + MORE, links.get(then, 0.0))
+            done = max(begin + rows / RATE, done + MORE)
+            links[then] = done
+        arrive[to, kind, i] = max(done + HOP, arrive.get((to, kind, i), 0.0))
+
+    def carry(role, op, i, now):
+        _, n, first_x, mode = pieces[i]
+        h = n // 2
+        if op == "y_send":
+            move(role, Y, n, now, role, Y, i)
+        elif op == "x_send":
+            move(role, X, h, now, role, X, i)
+        elif op == "x_first":
+            move(role, X, n, now, role, X, i)
+        elif op == "y_second":
+            move(role, Y, h, now, role, Y, i)
+        elif op == "z_in":
+            move(role, ZI, h, now, "inner", ZI, i)
+            if mode == 3:
+                move(role, ZI, h, now, "inner", ZF, i, ("inner", ZM))
+        elif op in ("z_mid", "z_own"):
+            move(role, ZM, h, now, role, ZM, i)
+        elif op == "z_out":
+            if mode == 3:
+                move(role, X, h, now, "outer", F, i, (role, ZO))
+            if mode != 2:
+                move(role, X, h, now, role, B, i)
+            move(role, ZO, h, now, "outer", ZO, i)
+        elif op == "relay":
+            move(role, X, h, now, role, B, i)
+        elif op == "forward":
+            to = "outer" if role == "inner" else "inner"
+            move(role, ZO if role == "inner" else ZI, h, now, to, F, i)
+
+    while True:
+        options = []
+        for role in ROLES:
+            clock = free.get(role, 0.0)
+            for op, i, kinds in todo[role]:
+                if all((role, kind, i) in arrive for kind in kinds):
+                    ready = max(arrive[role, kind, i] for kind in kinds)
+                    options.append((max(clock, ready), ready, role, op, i, kinds))
+            for op, link, deep in (("y_send", Y, DEEP_Y), ("x_first", X, DEEP_X)):
+                if starts[role][op]:
+                    ready = links.get((role, link), 0.0) - deep
+                    options.append((max(clock, ready), ready, role, op, starts[role][op][0], None))
+        if not options:
+            return out
+        now, _, role, op, i, kinds = min(options, key=lambda option: option[:2])
+        if kinds is None:
+            starts[role][op].pop(0)
+        else:
+            todo[role].remove((op, i, kinds))
+        out[role].append((now, op, i))
+        now += COST.get(op, 0.03)
+        free[role] = now
+        carry(role, op, i, now)
+        out["end"] = max(arrive.values())
+        out["links"] = links
 
 
 def fits(seq_count, dp_count):
-    depth = seq_count // 2
-    return dp_count == 2 * CORES and depth >= 2 and seq_count % 2 == 0 and depth & (depth - 1) == 0
+    return dp_count == 2 * CORES and seq_count == 2 * LINE
 
 
 def dot(a, b, da, db):
@@ -135,9 +252,9 @@
     x_ref, w_ref, xs_ref, xr_ref, xt_ref,
     st_ref, pair_ref, kvr_ref, qgr_ref, ox_ref, sxs_ref, sxr_ref,
     ls_ref, lr_ref, ups_ref, upr_ref, fg_ref,
-    ys_ref, yr_ref, acc_ref, xrs_ref, zs_ref, zr_ref, us_ref, ur_ref,
+    ys_ref, yr_ref, acc_ref, xrs_ref, zs_ref, zr_ref, zm_ref, zf_ref,
     load_sem, core_s, core_r, kv_s, kv_r, qg_s, qg_r, sx_s, sx_r,
-    y_s, y_r, x_s, x_r, z_s, z_r, b_s, b_r,
+    send_s, hop_r,
 ):
     seq = lax.axis_index("seq")
     dp = lax.axis_index("dp")
@@ -147,7 +264,8 @@
     across = {"seq": seq, "dp": (1 - y) * CORES + c}
     beside = {"seq": z * 2 + (1 - x), "dp": dp}
 
-    corner = {"seq": (z + 1 - 2 * (z % 2)) * 2 + (1 - x), "dp": dp}
+    near = jnp.where(z % 3 == 0, z + 1 - 2 * (z // 3), 3 * (z // 2))
+    diagonal = {"seq": near * 2 + (1 - x), "dp": dp}
 
     def along(other):
         return {"seq": other * 2 + x, "dp": dp}
@@ -158,7 +276,7 @@
     load_w.start()
 
     barrier = pltpu.get_barrier_semaphore()
-    friends = [mate, across, beside, corner] + [along(lax.rem(z + d, depth)) for d in range(1, depth)]
+    friends = [mate, across, beside, diagonal] + [along(lax.rem(z + d, depth)) for d in range(1, depth)]
     for friend in friends:
         pl.semaphore_signal(barrier, inc=1, device_id=friend, device_id_type=MESH)
 
@@ -232,6 +350,9 @@
     for part in range(2):
         cols = pl.ds(pl.multiple_of((part * CORES + c) * shard, 128), shard)
         xt_ref[part, :, 0:rows] = x_ref[:, cols].T
+
+    load_w.wait()
+    low = jnp.dot(x_ref[...], w_ref[...], preferred_element_type=jnp.float32).astype(jnp.bfloat16)
 
     collect(*scan_a, first)
     lead_sum = sxs_ref[:, first, :]
@@ -279,47 +400,115 @@
     low_copy.wait_recv()
     both = jnp.concatenate([low_grad, lr_ref[...].astype(jnp.bfloat16)], axis=0)
 
-    size = shard // CHUNKS
-    pieces = [(i * size, size) for i in range(CHUNKS)] + [(shard, ushard)]
+    pieces = cut(shard, ushard)
     count = len(pieces)
+    outer = (z == 0) | (z == depth - 1)
+    inner = jnp.logical_not(outer)
+    mid = jnp.where(z < depth // 2, depth // 2 - 1, depth // 2)
+    end = jnp.where(z < depth // 2, 0, depth - 1)
+    inward, outward, opposite = along(mid), along(end), along(depth - 1 - z)
+    further = along(depth - 1 - mid)
+    corner = {"seq": end * 2 + (1 - x), "dp": dp}
+    slots = landing(pieces)
+    sent = {}
+
+    def send(role, kind, i, src, dst, where):
+        rows = src.shape[0]
+        sent[kind] = sent.get(kind, 0) + rows
+        at = slots.get((kind, i), len(slots))
+        remote(src, dst, send_s.at[kind], hop_r.at[at], where).start()
+
+    def arrived(kind, i, like):
+        remote(like, like, send_s.at[kind], hop_r.at[slots[kind, i]], mate).wait_recv()
 
     def partial(i, part):
-        off, n = pieces[i]
+        off, n = pieces[i][:2]
         if off < shard:
             return jnp.dot(xt_ref[part, off : off + n, :], both, preferred_element_type=jnp.float32)
         mine = pl.ds(pl.multiple_of((part * CORES + c) * ushard, 8), ushard)
         return fg_ref[mine, :] + upr_ref[part]
 
     def half(i, which):
-        off, n = pieces[i]
+        off, n = pieces[i][:2]
         return pl.ds(pl.multiple_of(off + which * (n // 2), 8), n // 2)
 
-    def place(i, which, cuts):
-        off, n = pieces[i]
+    def short(i):
+        off, n = pieces[i][:2]
+        return slice(off // 2, off // 2 + n // 2)
+
+    def place(i, which):
+        off, n = pieces[i][:2]
         ref, base = (down_ref, off) if off < shard else (up_ref, 0)
-        return ref.at[pl.ds(pl.multiple_of(base + which * (n // cuts), 8), n // cuts), :]
-
-    y_copies, x_copies = [], []
-    b_copies = []
-    top = depth.bit_length() - 1
-    z_copies = [[] for _ in range(top)]
-    b = z % 2
-
-    def flip(level):
-        bit = 1 << level
-        return z + bit - 2 * bit * ((z // bit) % 2)
-
-    def y_stage(i):
-        off, n = pieces[i]
-        ys_ref[off : off + n, :] = partial(i, 1 - y)
-        copy = remote(ys_ref.at[off : off + n, :], yr_ref.at[off : off + n, :], y_s.at[i], y_r.at[i], across)
-        copy.start()
-        y_copies.append(copy)
-
-    for i in range(count - 1):
-        y_stage(i)
-    load_w.wait()
-    low = jnp.dot(x_ref[...], w_ref[...], preferred_element_type=jnp.float32).astype(jnp.bfloat16)
+        return ref.at[pl.ds(pl.multiple_of(base + which * (n // 2), 8), n // 2), :]
+
+    def perform(role, op, i):
+        off, n, first_x, mode = pieces[i]
+        h = n // 2
+        whole, low_half, high_half = slice(off, off + n), slice(off, off + h), slice(off + h, off + n)
+        small = short(i)
+        landed = Y if first_x else X
+        if op == "y_send":
+            if off >= shard:
+                up_copy.wait_recv()
+            ys_ref[whole, :] = partial(i, 1 - y)
+            send(role, Y, i, ys_ref.at[whole, :], yr_ref.at[whole, :], across)
+        elif op == "x_send":
+            own = partial(i, y)
+            arrived(Y, i, yr_ref.at[whole, :])
+            acc_ref[whole, :] = own + yr_ref[whole, :]
+            send(role, X, i, acc_ref.at[half(i, 1 - x), :], xrs_ref.at[small, :], beside)
+        elif op == "x_first":
+            ys_ref[whole, :] = partial(i, 1 - y)
+            send(role, X, i, ys_ref.at[half(i, 1 - x), :], yr_ref.at[high_half, :], beside)
+            acc_ref[whole, :] = partial(i, y)
+            send(role, X, i, acc_ref.at[half(i, 1 - x), :], yr_ref.at[low_half, :], beside)
+        elif op == "y_second":
+            arrived(X, i, yr_ref.at[whole, :])
+            ys_ref[half(i, x), :] += yr_ref[high_half, :]
+            send(role, Y, i, ys_ref.at[half(i, x), :], xrs_ref.at[small, :], across)
+            acc_ref[half(i, x), :] += yr_ref[low_half, :]
+        elif op == "z_in":
+            arrived(landed, i, xrs_ref.at[small, :])
+            zs_ref[small, :] = acc_ref[half(i, x), :] + xrs_ref[small, :]
+            send(role, ZI, i, zs_ref.at[small, :], zr_ref.at[small, :], inward)
+            if mode == 3:
+                send(role, ZF, i, zs_ref.at[small, :], zf_ref.at[small, :], further)
+        elif op == "z_own":
+            arrived(landed, i, xrs_ref.at[small, :])
+            zs_ref[small, :] = acc_ref[half(i, x), :] + xrs_ref[small, :]
+            send(role, ZM, i, zs_ref.at[small, :], zm_ref.at[small, :], opposite)
+        elif op == "z_mid":
+            arrived(landed, i, xrs_ref.at[small, :])
+            own = acc_ref[half(i, x), :] + xrs_ref[small, :]
+            arrived(ZI, i, zr_ref.at[small, :])
+            zs_ref[small, :] = own + zr_ref[small, :]
+            send(role, ZM, i, zs_ref.at[small, :], zm_ref.at[small, :], opposite)
+        elif op == "z_out":
+            own = zs_ref[small, :]
+            if mode == 3:
+                arrived(ZI, i, zr_ref.at[small, :])
+                own = own + zr_ref[small, :]
+            arrived(ZM, i, zm_ref.at[small, :])
+            own = own + zm_ref[small, :]
+            if mode == 3:
+                arrived(ZF, i, zf_ref.at[small, :])
+                own = own + zf_ref[small, :]
+            spot = place(i, x)
+            spot[...] = own * inverse
+            if mode == 3:
+                send(role, F, i, spot, spot, corner)
+            if mode in (0, 1, 3):
+                send(role, B, i, spot, spot, beside)
+            send(role, ZO, i, spot, spot, outward)
+        elif op == "relay":
+            spot = place(i, x)
+            arrived(ZO, i, spot)
+            send(role, B, i, spot, spot, beside)
+        elif op == "forward":
+            spot = place(i, 1 - x)
+            arrived(B, i, spot)
+            send(role, F, i, spot, spot, outward if role == "inner" else inward)
+
     up_all = dot(fg, low, 0, 0)
     fg_ref[...] = up_all
     for part in range(2):
@@ -328,65 +517,25 @@
     up_copy = remote(ups_ref, upr_ref, core_s.at[3], core_r.at[3], mate)
     up_copy.start()
 
-    up_copy.wait_recv()
-    y_stage(count - 1)
-
-    def x_stage(i):
-        off, n = pieces[i]
-        own = partial(i, y)
-        y_copies[i].wait_recv()
-        acc_ref[off : off + n, :] = own + yr_ref[off : off + n, :]
-        h = n // 2
-        short = pl.ds(off // 2, h)
-        copy = remote(acc_ref.at[half(i, 1 - x), :], xrs_ref.at[short, :], x_s.at[i], x_r.at[i], beside)
-        copy.start()
-        x_copies.append(copy)
-
-    def z_stage(i, level):
-        off, n = pieces[i]
-        h, e = n // 2, n // 4
-        if level == 0:
-            x_copies[i].wait_recv()
-            zs_ref[off // 2 : off // 2 + h, :] = acc_ref[half(i, x), :] + xrs_ref[off // 2 : off // 2 + h, :]
-            away = pl.ds(pl.multiple_of(off // 2 + (1 - b) * e, 8), e)
-            source, target = zs_ref.at[away, :], zr_ref.at[off // 4 : off // 4 + e, :]
-        else:
-            z_copies[level - 1][i].wait_recv()
-            short = slice(off // 4, off // 4 + e)
-            if level == 1:
-                kept = zs_ref[pl.ds(pl.multiple_of(off // 2 + b * e, 8), e), :] + zr_ref[short, :]
-            else:
-                kept = us_ref[level - 2, short, :] + ur_ref[level - 2, short, :]
-            if level == top:
-                spot = place(i, x * 2 + b, 4)
-                spot[...] = kept * inverse
-                for at, where in enumerate((beside, along(flip(0)), corner)):
-                    copy = remote(spot, place(i, x * 2 + b, 4), b_s.at[at, i], b_r.at[at, i], where)
-                    copy.start()
-                    b_copies.append(copy)
-                return
-            us_ref[level - 1, short, :] = kept
-            source, target = us_ref.at[level - 1, short, :], ur_ref.at[level - 1, short, :]
-        copy = remote(source, target, z_s.at[level, i], z_r.at[level, i], along(flip(level)))
-        copy.start()
-        z_copies[level].append(copy)
-
-    levels = top + 1
-    for t in range(count + levels * SKEW):
-        if t < count:
-            x_stage(t)
-        for level in range(levels):
-            i = t - SKEW * (1 + level)
-            if 0 <= i < count:
-                z_stage(i, level)
-
-    for copy in b_copies:
-        copy.wait_recv()
+    for role, here in (("outer", outer), ("inner", inner)):
+        @pl.when(here)
+        def _(role=role):
+            sent.clear()
+            for _, op, i in plan(pieces)[role]:
+                perform(role, op, i)
+            late = sum(n // 2 for _, n, _, mode in pieces if mode in (1, 3) and role == "outer") + sum(
+                n // 2 for _, n, _, mode in pieces if (role, mode) not in (("outer", 2), ("inner", 1)))
+            like = ys_ref.at[0:late, :]
+            remote(like, like, send_s.at[0], hop_r.at[len(slots)], mate).wait_recv()
+            for kind, rows in sent.items():
+                like = ys_ref.at[0:rows, :]
+                remote(like, like, send_s.at[kind], hop_r.at[len(slots)], mate).wait_send()
+
     for ups, downs in (scan_a, scan_b):
         for d in range(1, depth):
             pl.when(z + d < depth)(ups[d - 1].wait_send)
             pl.when(z >= d)(downs[d - 1].wait_send)
-    for copy in core_copies + [other, swap, low_copy, up_copy] + y_copies + x_copies + sum(z_copies, []) + b_copies:
+    for copy in core_copies + [other, swap, low_copy, up_copy]:
         copy.wait_send()
 
 
@@ -409,10 +558,8 @@
     factor = 1.0 / math.sqrt(HEAD_SIZE * length)
     inverse = 1.0 / math.sqrt(length * dp_count)
     depth = seq_count // 2
-    stages = depth.bit_length() - 1
     shard, ushard = model // dp_count, features // dp_count
     total = shard + ushard
-    count = CHUNKS + 1
     f32, bf16 = jnp.float32, jnp.bfloat16
     dma = pltpu.SemaphoreType.DMA
     vmem = pl.BlockSpec(memory_space=pltpu.VMEM)
@@ -423,7 +570,7 @@
     ]
     out = pl.pallas_call(
         functools.partial(fused_kernel, depth, factor, inverse),
-        out_shape=shapes,
+        out_shape=[pltpu.VMEM(part.shape, part.dtype) for part in shapes],
         in_specs=[hbm, hbm] + [vmem] * 5,
         out_specs=[vmem] * 5,
         scratch_shapes=[
@@ -449,15 +596,13 @@
             pltpu.VMEM((total, rank), f32),
             pltpu.VMEM((total // 2, rank), f32),
             pltpu.VMEM((total // 2, rank), f32),
-            pltpu.VMEM((total // 4, rank), f32),
-            pltpu.VMEM((max(stages - 1, 1), total // 4, rank), f32),
-            pltpu.VMEM((max(stages - 1, 1), total // 4, rank), f32),
+            pltpu.VMEM((total // 2, rank), f32),
+            pltpu.VMEM((total // 2, rank), f32),
+            pltpu.VMEM((total // 2, rank), f32),
             dma((2,)), dma((4,)), dma((4,)),
             dma((2 * depth - 2,)), dma((2 * depth - 2,)), dma((2 * depth - 2,)), dma((2 * depth - 2,)),
             dma((2,)), dma((2,)),
-            dma((count,)), dma((count,)), dma((count,)), dma((count,)),
-            dma((stages, count)), dma((stages, count)),
-            dma((3, count)), dma((3, count)),
+            dma((KINDS,)), dma((len(landing(cut(shard, ushard))) + 1,)),
         ],
         compiler_params=pltpu.CompilerParams(
             collective_id=0, has_side_effects=True
@@ -473,7 +618,7 @@
         in_specs=[vmem] * 5,
         out_specs=[hbm] * 5,
         scratch_shapes=[dma((5,))],
-    )(*out)
+    )(*[pltpu.with_memory_space_constraint(part, pltpu.VMEM) for part in out])
     return tuple(part.reshape(1, rows, width) for part in out[:3]) + tuple(out[3:])
 
 

time: 62.7 us -> 58.7 us (0.936)
  Pallas kernels: 61.8 us -> 57.9 us
    pallas_call x1, Pallas kernels: 59.5 us -> 56.9 us  [fast(): pl.pallas_call(functools.partial(fused_kernel, depth, factor, inverse), o...]
    pallas_call x1, Pallas kernels: 2.3 us -> 1.05 us  [fast(): pl.pallas_call(write_out, out_shape=shapes, in_specs=[vmem] * 5, out_spec...]
where the time goes in v1:
time: 58.7 us; the launch traced here: 58.6 us
  Pallas kernels  57.9 us (99%)
  between operations  0.64 us (1%)
    pallas_call x1, Pallas kernels, fast(): pl.pallas_call(functools.partial(fused_kernel, depth, factor, inverse), o...  56.9 us

profile of v1, /device:TPU:0, one launch (start us, length us, event | category | flops | bytes accessed | tf_op | source)
XLA Modules:
  0.0 58.6 jit_solution(14977071690815474257)
XLA Ops:
  0.6 56.9 %shard_map.110 = (bf16[128,128]{1,0:T(8,128)(2,1)S(1)}, bf16[128,128]{1,0:T(8,128)(2,1)S(1)}, bf16[128,128]{1,0:T(8,128)(2,1)S(1)}, f32[2048,128]{1,0:T(8,128)S(1)}, f32[96,128]{1,0:T(8,128)S(1)}) custom-call(bf16[128,8192]{1,0:T(8,128)(2,1)} %bitcast.8, bf16[8192,128]{1,0:T(8,128)(2,1)} %w_hbm.1, bf16[384,128]{1,0:T(8,128)(2,1)} %u_ref.1, ...), custom_call_target="tpu_custom_call" | custom-call | tf_op jit(solution)/shard_map/pallas_call | solution.py:571
  57.5 1.1 %shard_map.111 = (bf16[128,128]{1,0:T(8,128)(2,1)}, bf16[128,128]{1,0:T(8,128)(2,1)}, bf16[128,128]{1,0:T(8,128)(2,1)}, f32[2048,128]{1,0:T(8,128)}, f32[96,128]{1,0:T(8,128)}) custom-call(bf16[128,128]{1,0:T(8,128)(2,1)S(1)} %get-tuple-element.15.refs_0_, bf16[128,128]{1,0:T(8,128)(2,1)S(1)} %get-tuple-element.16.refs_1_, ...), custom_call_target="tpu_custom_call" | custom-call | tf_op jit(solution)/shard_map/pallas_call | solution.py:615

commit v2 on v1

--- a/solution.py
+++ b/solution.py
@@ -116,37 +116,57 @@
 MESH = pl.DeviceIdType.MESH
 CORES = 2
 LINE = 4
-KINDS = 8
-Y, X, ZI, ZM, ZF, ZO, B, F = range(KINDS)
+KINDS = 9
+Y, X, ZI, ZM, ZF, ZO, B, F, ZL = range(KINDS)
 ROLES = ("outer", "inner")
-PIECES = 16
-UP_AT = 8
-X_FIRST = (0, 1, 2, 3)
-RELAYED = (2, 2, 2, 2, 2, 2, 2, 1, 1, 1, 1, 1, 1, 0, 3, 3, 3)
-RATE, HOP, MORE = 92.0, 1.75, 0.75
-DEEP_Y, DEEP_X = 2.0, 1.0
-COST = {"y_send": 0.17, "x_send": 0.18, "x_first": 0.32}
+CUTS = (
+    (14, 1, 2), (14, 1, 0), (16, 0, 0), (7, 1, 2), (5, 1, 0), (2, 0, 2), (12, 0, 2), (11, 0, 2),
+    (6, 0, 0), (7, 0, 2), (6, 1, 0), (4, 0, 1), (6, 1, 1), (7, 1, 0), (2, 1, 1), (2, 1, 1),
+    (0, 0, 0), (5, 1, 3), (2, 0, 0),
+)
+RATE, HOP, MORE, EARLY = 92.0, 1.75, 0.75, 4.3
+DEEP = (2.5, 0.3, 1.0)
+COST = {"y_send": 0.17, "x_send": 0.18, "x_first": 0.32, "z_first": 0.32, "z_join": 0.34, "p_send": 0.25}
 
 
 def cut(shard, ushard):
-    size = shard // PIECES
-    spans = [(i * size, size) for i in range(PIECES)]
-    spans.insert(UP_AT, (shard, ushard))
-    return [(off, n, i in X_FIRST, RELAYED[i]) for i, (off, n) in enumerate(spans)]
+    unit = shard // sum(parts for parts, _, _ in CUTS)
+    places, off = {}, 0
+    for i in sorted(range(len(CUTS)), key=lambda i: CUTS[i][1] != 2):
+        places[i] = off
+        off += CUTS[i][0] * unit
+    return [
+        (places[i], parts * unit, color, mode) if parts else (shard, ushard, color, mode)
+        for i, (parts, color, mode) in enumerate(CUTS)
+    ]
+
+
+def fetched(pieces):
+    return sum(n for _, n, color, _ in pieces if color == 2)
+
+
+def working(color):
+    return {3: ("inner",), 5: ("inner",), 4: ("outer",), 6: ("outer",)}.get(color, ROLES)
+
+
+def direct(color, mode):
+    return mode == 3 and color < 3
 
 
 def landing(pieces):
     slots = {}
-    for i, (_, _, _, mode) in enumerate(pieces):
+    for i, (_, _, color, mode) in enumerate(pieces):
         for kind in (Y, X, ZI, ZM):
             slots[kind, i] = len(slots)
+        if color >= 3:
+            slots[ZL, i] = len(slots)
         if mode in (0, 2):
             slots[ZO, i] = slots[ZI, i]
         if mode == 1:
             slots[B, i] = len(slots)
         if mode == 2:
             slots[B, i] = slots[ZM, i]
-        if mode == 3:
+        if direct(color, mode):
             slots[ZF, i] = len(slots)
     return slots
 
@@ -155,21 +175,39 @@
     free, links, arrive = {}, {}, {}
     out = {role: [] for role in ROLES}
     todo = {role: [] for role in ROLES}
-    starts = {role: {"y_send": [], "x_first": []} for role in ROLES}
-    for i, (_, _, first_x, mode) in enumerate(pieces):
+    starts = {role: {"y_send": [], "x_first": [], "z_first": []} for role in ROLES}
+    early = any(color == 2 for _, _, color, _ in pieces)
+    for i, (_, _, color, mode) in enumerate(pieces):
+        first_x = color in (1, 5, 6)
         landed = Y if first_x else X
-        for role in ROLES:
-            starts[role]["x_first" if first_x else "y_send"].append(i)
+        for role in working(color):
+            if color == 2:
+                arrive[role, "P", i] = EARLY
+                todo[role].append(("p_send", i, ("P",)))
+                continue
+            if color >= 3:
+                todo[role].append(("z_join", i, (ZL,)))
+                starts["outer" if role == "inner" else "inner"]["z_first"].append(i)
+            else:
+                starts[role]["x_first" if first_x else "y_send"].append(i)
             todo[role].append(("y_second", i, (X,)) if first_x else ("x_send", i, (Y,)))
-        todo["outer"].append(("z_in", i, (landed,)))
-        if mode == 3:
+        if "outer" in working(color):
+            todo["outer"].append(("z_in", i, (landed,)))
+        needs = (landed,) * ("inner" in working(color)) + (ZI,) * ("outer" in working(color))
+        if direct(color, mode):
             todo["inner"] += [("z_own", i, (landed,)), ("z_out", i, (ZI, ZM, ZF))]
         else:
-            todo["inner"] += [("z_mid", i, (landed, ZI)), ("z_out", i, (ZM,))]
+            todo["inner"] += [("z_mid", i, needs), ("z_out", i, (ZM,))]
         if mode in (0, 2):
             todo["outer"].append(("relay", i, (ZO,)))
         if mode in (1, 2):
             todo["inner" if mode == 1 else "outer"].append(("forward", i, (B,)))
+    if early:
+        for role in ROLES:
+            links[role, Y] = 128 / RATE
+            arrive[role, "L", 0] = EARLY - 1.1
+            arrive[role, "G", 0] = EARLY - 0.1
+            todo[role] += [("p_low", 0, ("L",)), ("p_get", 0, ("G",))]
 
     def move(role, link, rows, now, to, kind, i, then=None):
         begin = max(now, links.get((role, link), 0.0))
@@ -182,19 +220,22 @@
         arrive[to, kind, i] = max(done + HOP, arrive.get((to, kind, i), 0.0))
 
     def carry(role, op, i, now):
-        _, n, first_x, mode = pieces[i]
+        _, n, color, mode = pieces[i]
         h = n // 2
-        if op == "y_send":
+        first_x = color in (1, 5, 6)
+        if op == "z_first":
+            move(role, ZI if role == "outer" else ZO, 2 * n, now, "inner" if role == "outer" else "outer", ZL, i)
+        elif op == "y_send" or (op == "z_join" and not first_x):
             move(role, Y, n, now, role, Y, i)
-        elif op == "x_send":
+        elif op in ("x_send", "p_send"):
             move(role, X, h, now, role, X, i)
-        elif op == "x_first":
+        elif op == "x_first" or op == "z_join":
             move(role, X, n, now, role, X, i)
         elif op == "y_second":
             move(role, Y, h, now, role, Y, i)
         elif op == "z_in":
             move(role, ZI, h, now, "inner", ZI, i)
-            if mode == 3:
+            if direct(color, mode):
                 move(role, ZI, h, now, "inner", ZF, i, ("inner", ZM))
         elif op in ("z_mid", "z_own"):
             move(role, ZM, h, now, role, ZM, i)
@@ -218,7 +259,8 @@
                 if all((role, kind, i) in arrive for kind in kinds):
                     ready = max(arrive[role, kind, i] for kind in kinds)
                     options.append((max(clock, ready), ready, role, op, i, kinds))
-            for op, link, deep in (("y_send", Y, DEEP_Y), ("x_first", X, DEEP_X)):
+            side = ZI if role == "outer" else ZO
+            for op, link, deep in (("y_send", Y, DEEP[0]), ("x_first", X, DEEP[1]), ("z_first", side, DEEP[2])):
                 if starts[role][op]:
                     ready = links.get((role, link), 0.0) - deep
                     options.append((max(clock, ready), ready, role, op, starts[role][op][0], None))
@@ -247,13 +289,14 @@
 
 def fused_kernel(
     depth, factor, inverse,
-    x_hbm, w_hbm, u_ref, q_ref, k_ref, v_ref, g_ref,
+    x_hbm, w_hbm, u_hbm, q_hbm, k_hbm, v_hbm, g_hbm,
     qo_ref, ko_ref, vo_ref, down_ref, up_ref,
-    x_ref, w_ref, xs_ref, xr_ref, xt_ref,
+    x_ref, w_ref, u_ref, four_ref, xs_ref, xr_ref, xt_ref,
     st_ref, pair_ref, kvr_ref, qgr_ref, ox_ref, sxs_ref, sxr_ref,
     ls_ref, lr_ref, ups_ref, upr_ref, fg_ref,
-    ys_ref, yr_ref, acc_ref, xrs_ref, zs_ref, zr_ref, zm_ref, zf_ref,
-    load_sem, core_s, core_r, kv_s, kv_r, qg_s, qg_r, sx_s, sx_r,
+    ys_ref, yr_ref, acc_ref, xrs_ref, zs_ref, zr_ref, zm_ref, zf_ref, zl_ref,
+    ps_ref, pr_ref, pt_ref, lo_ref, them_ref, pre_s, pre_r,
+    load_sem, core_s, core_r, scan_s, scan_r, sx_s, sx_r,
     send_s, hop_r,
 ):
     seq = lax.axis_index("seq")
@@ -262,6 +305,7 @@
     y, c = dp // CORES, dp % CORES
     mate = {"seq": seq, "dp": y * CORES + (1 - c)}
     across = {"seq": seq, "dp": (1 - y) * CORES + c}
+    apart = {"seq": seq, "dp": (1 - y) * CORES + (1 - c)}
     beside = {"seq": z * 2 + (1 - x), "dp": dp}
 
     near = jnp.where(z % 3 == 0, z + 1 - 2 * (z // 3), 3 * (z // 2))
@@ -270,21 +314,27 @@
     def along(other):
         return {"seq": other * 2 + x, "dp": dp}
 
+    for i, part in enumerate((q_hbm, k_hbm, v_hbm, g_hbm)):
+        pltpu.make_async_copy(part, four_ref.at[i], load_sem.at[2]).start()
+    load_u = pltpu.make_async_copy(u_hbm, u_ref, load_sem.at[3])
     load_x = pltpu.make_async_copy(x_hbm, x_ref, load_sem.at[0])
     load_w = pltpu.make_async_copy(w_hbm, w_ref, load_sem.at[1])
+    load_u.start()
     load_x.start()
     load_w.start()
 
     barrier = pltpu.get_barrier_semaphore()
-    friends = [mate, across, beside, diagonal] + [along(lax.rem(z + d, depth)) for d in range(1, depth)]
+    friends = [mate, across, apart, beside, diagonal] + [along(lax.rem(z + d, depth)) for d in range(1, depth)]
     for friend in friends:
         pl.semaphore_signal(barrier, inc=1, device_id=friend, device_id_type=MESH)
 
-    rows = q_ref.shape[0]
+    rows, width = qo_ref.shape
     shard = down_ref.shape[0]
     ushard = up_ref.shape[0]
-    width = q_ref.shape[1]
-    q, k, v, g = q_ref[...], k_ref[...], v_ref[...], g_ref[...]
+    pieces = cut(shard, ushard)
+    early = fetched(pieces)
+    pltpu.make_async_copy(four_ref, four_ref, load_sem.at[2]).wait()
+    q, k, v, g = four_ref[0], four_ref[1], four_ref[2], four_ref[3]
     st_ref[0] = dot(k, v, 0, 0)
     st_ref[1] = dot(q, g, 0, 0)
     pl.semaphore_wait(barrier, len(friends))
@@ -303,8 +353,9 @@
         ups, downs = [], []
         for d in range(1, depth):
             slot = at * (depth - 1) + d - 1
-            ups.append(remote(source.at[0, part, :], kvr_ref.at[d - 1, part, :], kv_s.at[slot], kv_r.at[slot], along(lax.rem(z + d, depth))))
-            downs.append(remote(source.at[1, part, :], qgr_ref.at[d - 1, part, :], qg_s.at[slot], qg_r.at[slot], along(lax.rem(z - d + depth, depth))))
+            back = at * (depth - 1) + depth - d - 1
+            ups.append(remote(source.at[0, part, :], kvr_ref.at[d - 1, part, :], scan_s.at[0], scan_r.at[slot], along(lax.rem(z + d, depth))))
+            downs.append(remote(source.at[1, part, :], qgr_ref.at[d - 1, part, :], scan_s.at[0], scan_r.at[back], along(lax.rem(z - d + depth, depth))))
         for d in range(1, depth):
             pl.when(z + d < depth)(ups[d - 1].start)
             pl.when(z >= d)(downs[d - 1].start)
@@ -326,7 +377,14 @@
     scan_a = scan(st_ref, first, 0)
 
     load_x.wait()
-    core_copies = []
+    core_copies, extra = [], []
+    if early:
+        for at, where, core in ((0, across, c), (1, apart, 1 - c)):
+            cols = pl.ds(pl.multiple_of(((1 - y) * CORES + core) * shard, 128), early)
+            ps_ref[at] = x_ref[:, cols].astype(jnp.float32)
+            copy = remote(ps_ref.at[at], pr_ref.at[at], pre_s.at[at], pre_r.at[at], where)
+            copy.start()
+            extra.append(copy)
     for part in range(2):
         cols = pl.ds(pl.multiple_of((part * CORES + 1 - c) * shard, 128), shard)
         xs_ref[part] = x_ref[:, cols].astype(jnp.float32)
@@ -389,10 +447,16 @@
     k_grad = (factor * (k_in + dot(v, suffix, 1, 1))).astype(jnp.bfloat16)
     v_grad = (factor * (v_in + dot(k, suffix, 1, 0))).astype(jnp.bfloat16)
     fg = jnp.concatenate([q_grad, k_grad, v_grad], axis=1)
+    load_u.wait()
     low_grad = dot(fg, u_ref[...], 1, 0).astype(jnp.bfloat16)
     ls_ref[...] = low_grad.astype(jnp.float32)
     low_copy = remote(ls_ref, lr_ref, core_s.at[2], core_r.at[2], mate)
     low_copy.start()
+    if early:
+        low_across = remote(ls_ref, lo_ref.at[0], pre_s.at[2], pre_r.at[2], across)
+        low_across.start()
+        low_apart = remote(lo_ref.at[0], lo_ref.at[1], pre_s.at[3], pre_r.at[3], mate)
+        extra.extend([low_across, low_apart])
     qo_ref[...] = q_grad
     ko_ref[...] = k_grad
     vo_ref[...] = v_grad
@@ -400,8 +464,6 @@
     low_copy.wait_recv()
     both = jnp.concatenate([low_grad, lr_ref[...].astype(jnp.bfloat16)], axis=0)
 
-    pieces = cut(shard, ushard)
-    count = len(pieces)
     outer = (z == 0) | (z == depth - 1)
     inner = jnp.logical_not(outer)
     mid = jnp.where(z < depth // 2, depth // 2 - 1, depth // 2)
@@ -413,8 +475,7 @@
     sent = {}
 
     def send(role, kind, i, src, dst, where):
-        rows = src.shape[0]
-        sent[kind] = sent.get(kind, 0) + rows
+        sent[kind] = sent.get(kind, 0) + src.shape[0]
         at = slots.get((kind, i), len(slots))
         remote(src, dst, send_s.at[kind], hop_r.at[at], where).start()
 
@@ -442,8 +503,10 @@
         return ref.at[pl.ds(pl.multiple_of(base + which * (n // 2), 8), n // 2), :]
 
     def perform(role, op, i):
-        off, n, first_x, mode = pieces[i]
+        off, n, color, mode = pieces[i]
         h = n // 2
+        first_x = color in (1, 5, 6)
+        workers = working(color)
         whole, low_half, high_half = slice(off, off + n), slice(off, off + h), slice(off + h, off + n)
         small = short(i)
         landed = Y if first_x else X
@@ -452,8 +515,39 @@
                 up_copy.wait_recv()
             ys_ref[whole, :] = partial(i, 1 - y)
             send(role, Y, i, ys_ref.at[whole, :], yr_ref.at[whole, :], across)
+        elif op == "z_first":
+            where = inward if role == "outer" else outward
+            ys_ref[whole, :] = partial(i, 1 - y)
+            send(role, ZL, i, ys_ref.at[whole, :], zl_ref.at[0, whole, :], where)
+            acc_ref[whole, :] = partial(i, y)
+            send(role, ZL, i, acc_ref.at[whole, :], zl_ref.at[1, whole, :], where)
+        elif op == "z_join":
+            arrived(ZL, i, zl_ref.at[:, whole, :])
+            ys_ref[whole, :] = partial(i, 1 - y) + zl_ref[0, whole, :]
+            if first_x:
+                send(role, X, i, ys_ref.at[half(i, 1 - x), :], yr_ref.at[high_half, :], beside)
+                acc_ref[whole, :] = partial(i, y) + zl_ref[1, whole, :]
+                send(role, X, i, acc_ref.at[half(i, 1 - x), :], yr_ref.at[low_half, :], beside)
+            else:
+                send(role, Y, i, ys_ref.at[whole, :], yr_ref.at[whole, :], across)
+        elif op == "p_low":
+            low_across.wait_recv()
+            low_apart.start()
+        elif op == "p_get":
+            low_apart.wait_recv()
+            for at in range(2):
+                extra[at].wait_recv()
+                pt_ref[:, at * rows : (at + 1) * rows] = pr_ref[at].astype(jnp.bfloat16).T
+                them_ref[at * rows : (at + 1) * rows, :] = lo_ref[at].astype(jnp.bfloat16)
+        elif op == "p_send":
+            acc_ref[whole, :] = partial(i, y) + jnp.dot(
+                pt_ref[whole, :], them_ref[...], preferred_element_type=jnp.float32
+            )
+            send(role, X, i, acc_ref.at[half(i, 1 - x), :], xrs_ref.at[small, :], beside)
         elif op == "x_send":
             own = partial(i, y)
+            if color >= 3:
+                own = own + zl_ref[1, whole, :]
             arrived(Y, i, yr_ref.at[whole, :])
             acc_ref[whole, :] = own + yr_ref[whole, :]
             send(role, X, i, acc_ref.at[half(i, 1 - x), :], xrs_ref.at[small, :], beside)
@@ -471,26 +565,29 @@
             arrived(landed, i, xrs_ref.at[small, :])
             zs_ref[small, :] = acc_ref[half(i, x), :] + xrs_ref[small, :]
             send(role, ZI, i, zs_ref.at[small, :], zr_ref.at[small, :], inward)
-            if mode == 3:
+            if direct(color, mode):
                 send(role, ZF, i, zs_ref.at[small, :], zf_ref.at[small, :], further)
         elif op == "z_own":
             arrived(landed, i, xrs_ref.at[small, :])
             zs_ref[small, :] = acc_ref[half(i, x), :] + xrs_ref[small, :]
             send(role, ZM, i, zs_ref.at[small, :], zm_ref.at[small, :], opposite)
         elif op == "z_mid":
-            arrived(landed, i, xrs_ref.at[small, :])
-            own = acc_ref[half(i, x), :] + xrs_ref[small, :]
-            arrived(ZI, i, zr_ref.at[small, :])
-            zs_ref[small, :] = own + zr_ref[small, :]
+            if "inner" in workers:
+                arrived(landed, i, xrs_ref.at[small, :])
+                own = acc_ref[half(i, x), :] + xrs_ref[small, :]
+            if "outer" in workers:
+                arrived(ZI, i, zr_ref.at[small, :])
+                own = own + zr_ref[small, :] if "inner" in workers else zr_ref[small, :]
+            zs_ref[small, :] = own
             send(role, ZM, i, zs_ref.at[small, :], zm_ref.at[small, :], opposite)
         elif op == "z_out":
             own = zs_ref[small, :]
-            if mode == 3:
+            if direct(color, mode):
                 arrived(ZI, i, zr_ref.at[small, :])
                 own = own + zr_ref[small, :]
             arrived(ZM, i, zm_ref.at[small, :])
             own = own + zm_ref[small, :]
-            if mode == 3:
+            if direct(color, mode):
                 arrived(ZF, i, zf_ref.at[small, :])
                 own = own + zf_ref[small, :]
             spot = place(i, x)
@@ -527,15 +624,12 @@
                 n // 2 for _, n, _, mode in pieces if (role, mode) not in (("outer", 2), ("inner", 1)))
             like = ys_ref.at[0:late, :]
             remote(like, like, send_s.at[0], hop_r.at[len(slots)], mate).wait_recv()
-            for kind, rows in sent.items():
-                like = ys_ref.at[0:rows, :]
+            for kind, rows in list(sent.items()):
+                like = zl_ref.at[:, 0 : rows // 2, :] if kind == ZL else ys_ref.at[0:rows, :]
                 remote(like, like, send_s.at[kind], hop_r.at[len(slots)], mate).wait_send()
 
-    for ups, downs in (scan_a, scan_b):
-        for d in range(1, depth):
-            pl.when(z + d < depth)(ups[d - 1].wait_send)
-            pl.when(z >= d)(downs[d - 1].wait_send)
-    for copy in core_copies + [other, swap, low_copy, up_copy]:
+    remote(kvr_ref, kvr_ref, scan_s.at[0], scan_r.at[0], mate).wait_send()
+    for copy in core_copies + [other, swap, low_copy, up_copy] + extra:
         copy.wait_send()
 
 
@@ -560,6 +654,8 @@
     depth = seq_count // 2
     shard, ushard = model // dp_count, features // dp_count
     total = shard + ushard
+    pieces = cut(shard, ushard)
+    early = max(fetched(pieces), rows)
     f32, bf16 = jnp.float32, jnp.bfloat16
     dma = pltpu.SemaphoreType.DMA
     vmem = pl.BlockSpec(memory_space=pltpu.VMEM)
@@ -571,11 +667,13 @@
     out = pl.pallas_call(
         functools.partial(fused_kernel, depth, factor, inverse),
         out_shape=[pltpu.VMEM(part.shape, part.dtype) for part in shapes],
-        in_specs=[hbm, hbm] + [vmem] * 5,
+        in_specs=[hbm] * 7,
         out_specs=[vmem] * 5,
         scratch_shapes=[
             pltpu.VMEM((rows, model), bf16),
             pltpu.VMEM((model, rank), bf16),
+            pltpu.VMEM((features, rank), bf16),
+            pltpu.VMEM((4, rows, width), bf16),
             pltpu.VMEM((2, rows, shard), f32),
             pltpu.VMEM((2, rows, shard), f32),
             pltpu.VMEM((2, shard, 2 * rows), bf16),
@@ -599,10 +697,17 @@
             pltpu.VMEM((total // 2, rank), f32),
             pltpu.VMEM((total // 2, rank), f32),
             pltpu.VMEM((total // 2, rank), f32),
-            dma((2,)), dma((4,)), dma((4,)),
-            dma((2 * depth - 2,)), dma((2 * depth - 2,)), dma((2 * depth - 2,)), dma((2 * depth - 2,)),
+            pltpu.VMEM((2, total, rank), f32),
+            pltpu.VMEM((2, rows, early), f32),
+            pltpu.VMEM((2, rows, early), f32),
+            pltpu.VMEM((early, 2 * rows), bf16),
+            pltpu.VMEM((2, rows, rank), f32),
+            pltpu.VMEM((2 * rows, rank), bf16),
+            dma((4,)), dma((4,)),
+            dma((4,)), dma((4,)), dma((4,)),
+            dma((1,)), dma((2 * depth - 2,)),
             dma((2,)), dma((2,)),
-            dma((KINDS,)), dma((len(landing(cut(shard, ushard))) + 1,)),
+            dma((KINDS,)), dma((len(landing(pieces)) + 1,)),
         ],
         compiler_params=pltpu.CompilerParams(
             collective_id=0, has_side_effects=True

time: 58.7 us -> 53.3 us (0.908)
  Pallas kernels: 57.9 us -> 52.5 us
    pallas_call x1, Pallas kernels: 56.9 us -> 51.5 us  [fast(): pl.pallas_call(functools.partial(fused_kernel, depth, factor, inverse), o...]
where the time goes in v2:
time: 53.3 us; the launch traced here: 53.2 us
  Pallas kernels  52.5 us (98%)
  between operations  0.64 us (1%)
    pallas_call x1, Pallas kernels, fast(): pl.pallas_call(functools.partial(fused_kernel, depth, factor, inverse), o...  51.5 us

profile of v2, /device:TPU:0, one launch (start us, length us, event | category | flops | bytes accessed | tf_op | source)
XLA Modules:
  0.0 53.2 jit_solution(3388088691435270159)
XLA Ops:
  0.6 51.5 %shard_map.110 = (bf16[128,128]{1,0:T(8,128)(2,1)S(1)}, bf16[128,128]{1,0:T(8,128)(2,1)S(1)}, bf16[128,128]{1,0:T(8,128)(2,1)S(1)}, f32[2048,128]{1,0:T(8,128)S(1)}, f32[96,128]{1,0:T(8,128)S(1)}) custom-call(bf16[128,8192]{1,0:T(8,128)(2,1)} %bitcast.8, bf16[8192,128]{1,0:T(8,128)(2,1)} %w_hbm.1, bf16[384,128]{1,0:T(8,128)(2,1)} %u_hbm.1, ...), custom_call_target="tpu_custom_call" | custom-call | tf_op jit(solution)/shard_map/pallas_call | solution.py:667
  52.1 1.1 %shard_map.111 = (bf16[128,128]{1,0:T(8,128)(2,1)}, bf16[128,128]{1,0:T(8,128)(2,1)}, bf16[128,128]{1,0:T(8,128)(2,1)}, f32[2048,128]{1,0:T(8,128)}, f32[96,128]{1,0:T(8,128)}) custom-call(bf16[128,128]{1,0:T(8,128)(2,1)S(1)} %get-tuple-element.15.refs_0_, bf16[128,128]{1,0:T(8,128)(2,1)S(1)} %get-tuple-element.16.refs_1_, ...), custom_call_target="tpu_custom_call" | custom-call | tf_op jit(solution)/shard_map/pallas_call | solution.py:720

commit v3 on v2

--- a/solution.py
+++ b/solution.py
@@ -120,12 +120,12 @@
 Y, X, ZI, ZM, ZF, ZO, B, F, ZL = range(KINDS)
 ROLES = ("outer", "inner")
 CUTS = (
-    (14, 1, 2), (14, 1, 0), (16, 0, 0), (7, 1, 2), (5, 1, 0), (2, 0, 2), (12, 0, 2), (11, 0, 2),
-    (6, 0, 0), (7, 0, 2), (6, 1, 0), (4, 0, 1), (6, 1, 1), (7, 1, 0), (2, 1, 1), (2, 1, 1),
-    (0, 0, 0), (5, 1, 3), (2, 0, 0),
+    (6, 5, 2), (9, 3, 0), (6, 0, 0), (7, 1, 2), (2, 1, 0), (3, 6, 0), (5, 0, 0), (9, 1, 0),
+    (5, 0, 0), (8, 4, 0), (7, 4, 0), (7, 1, 2), (3, 6, 1), (5, 0, 0), (6, 3, 0), (3, 0, 0),
+    (5, 6, 3), (2, 0, 0), (8, 0, 0), (0, 0, 2), (3, 1, 0), (6, 1, 2), (5, 4, 3), (8, 1, 0),
 )
 RATE, HOP, MORE, EARLY = 92.0, 1.75, 0.75, 4.3
-DEEP = (2.5, 0.3, 1.0)
+DEEP = (2.0, 0.7, 2.0)
 COST = {"y_send": 0.17, "x_send": 0.18, "x_first": 0.32, "z_first": 0.32, "z_join": 0.34, "p_send": 0.25}
 
 

time: 53.3 us -> 50.2 us (0.942)
  Pallas kernels: 52.5 us -> 49.4 us
    pallas_call x1, Pallas kernels: 51.5 us -> 48.4 us  [fast(): pl.pallas_call(functools.partial(fused_kernel, depth, factor, inverse), o...]
where the time goes in v3:
time: 50.2 us; the launch traced here: 50 us
  Pallas kernels  49.4 us (98%)
  between operations  0.64 us (1%)
    pallas_call x1, Pallas kernels, fast(): pl.pallas_call(functools.partial(fused_kernel, depth, factor, inverse), o...  48.4 us
    pallas_call x1, Pallas kernels, fast(): pl.pallas_call(write_out, out_shape=shapes, in_specs=[vmem] * 5, out_spec...  1.05 us

profile of v3, /device:TPU:0, one launch (start us, length us, event | category | flops | bytes accessed | tf_op | source)
XLA Modules:
  0.0 50.0 jit_solution(3929852198149196003)
XLA Ops:
  0.6 48.4 %shard_map.110 = (bf16[128,128]{1,0:T(8,128)(2,1)S(1)}, bf16[128,128]{1,0:T(8,128)(2,1)S(1)}, bf16[128,128]{1,0:T(8,128)(2,1)S(1)}, f32[2048,128]{1,0:T(8,128)S(1)}, f32[96,128]{1,0:T(8,128)S(1)}) custom-call(bf16[128,8192]{1,0:T(8,128)(2,1)} %bitcast.8, bf16[8192,128]{1,0:T(8,128)(2,1)} %w_hbm.1, bf16[384,128]{1,0:T(8,128)(2,1)} %u_hbm.1, ...), custom_call_target="tpu_custom_call" | custom-call | tf_op jit(solution)/shard_map/pallas_call | solution.py:667
  49.0 1.1 %shard_map.111 = (bf16[128,128]{1,0:T(8,128)(2,1)}, bf16[128,128]{1,0:T(8,128)(2,1)}, bf16[128,128]{1,0:T(8,128)(2,1)}, f32[2048,128]{1,0:T(8,128)}, f32[96,128]{1,0:T(8,128)}) custom-call(bf16[128,128]{1,0:T(8,128)(2,1)S(1)} %get-tuple-element.15.refs_0_, bf16[128,128]{1,0:T(8,128)(2,1)S(1)} %get-tuple-element.16.refs_1_, ...), custom_call_target="tpu_custom_call" | custom-call | tf_op jit(solution)/shard_map/pallas_call | solution.py:720

commit v4 on v3

--- a/solution.py
+++ b/solution.py
@@ -116,37 +116,86 @@
 MESH = pl.DeviceIdType.MESH
 CORES = 2
 LINE = 4
-KINDS = 9
-Y, X, ZI, ZM, ZF, ZO, B, F, ZL = range(KINDS)
-ROLES = ("outer", "inner")
+KINDS = 10
+Y, X, ZI, ZM, ZF, ZO, B, F, ZL, D = range(KINDS)
+OPS = (
+    "y_send", "x_send", "x_first", "y_second", "z_first", "z_join", "z_in", "z_own", "z_mid",
+    "z_out", "relay", "forward", "p_low", "p_get", "p_send", "far", "near",
+)
+UNITS = 128
 CUTS = (
-    (6, 5, 2), (9, 3, 0), (6, 0, 0), (7, 1, 2), (2, 1, 0), (3, 6, 0), (5, 0, 0), (9, 1, 0),
-    (5, 0, 0), (8, 4, 0), (7, 4, 0), (7, 1, 2), (3, 6, 1), (5, 0, 0), (6, 3, 0), (3, 0, 0),
-    (5, 6, 3), (2, 0, 0), (8, 0, 0), (0, 0, 2), (3, 1, 0), (6, 1, 2), (5, 4, 3), (8, 1, 0),
+    (
+        (3, 3, 0, 0), (7, 5, 2, 0), (5, 4, 1, 0), (4, 0, 3, 0), (2, 0, 2, 0), (3, 0, 2, 0),
+        (7, 6, 0, 0), (0, 0, 0, 0), (3, 2, 0, 0), (3, 2, 0, 0), (3, 1, 0, 0), (7, 0, 0, 0),
+        (5, 6, 0, 0), (3, 1, 3, 0), (2, 0, 1, 0), (11, 0, 0, 0), (3, 4, 0, 0), (6, 3, 0, 0),
+        (3, 0, 0, 0), (12, 2, 0, 0),
+    ),
+    (
+        (10, 6, 0, 1), (14, 6, 1, 0), (6, 4, 1, 0), (2, 2, 2, 0), (3, 6, 1, 0), (9, 2, 2, 0),
+        (10, 1, 0, 0), (16, 0, 0, 1), (2, 3, 3, 0), (5, 2, 0, 0), (5, 0, 0, 0), (5, 1, 0, 1),
+        (4, 6, 0, 0), (5, 6, 0, 0), (9, 3, 2, 0), (9, 4, 3, 0), (3, 0, 0, 0), (0, 0, 0, 0),
+        (3, 2, 2, 0), (2, 5, 0, 0), (2, 0, 2, 0), (15, 1, 2, 0), (4, 2, 2, 0), (5, 5, 2, 1),
+        (16, 0, 0, 0),
+    ),
 )
-RATE, HOP, MORE, EARLY = 92.0, 1.75, 0.75, 4.3
-DEEP = (2.0, 0.7, 2.0)
-COST = {"y_send": 0.17, "x_send": 0.18, "x_first": 0.32, "z_first": 0.32, "z_join": 0.34, "p_send": 0.25}
-
-
-def cut(shard, ushard):
-    unit = shard // sum(parts for parts, _, _ in CUTS)
+ORDERS = (
+    (
+        512, 266, 513, 269, 3, 4, 5, 7, 11, 529, 14, 15, 394, 1536, 397, 642, 1664, 1800, 1801, 1811,
+        131, 132, 133, 135, 18, 139, 646, 142, 776, 777, 652, 143, 787, 778, 771, 781, 772, 773, 656, 775,
+        130, 779, 146, 390, 782, 396, 144, 783, 770, 786, 774, 780, 784, 1288, 1289, 1280, 1299, 1290, 1281, 1284,
+        1285, 1297, 1287, 1291, 1409, 1412, 1413, 1295, 1298, 1286, 1292, 1296,
+    ),
+    (
+        520, 526, 531, 535, 262, 267, 277, 7, 1536, 1664, 1795, 1797, 1801, 1810, 1814, 390, 395, 405, 771, 640,
+        773, 135, 777, 10, 786, 790, 16, 774, 17, 779, 20, 24, 789, 641, 384, 138, 144, 642, 145, 148,
+        644, 775, 652, 152, 653, 768, 385, 778, 784, 130, 785, 788, 655, 1283, 388, 396, 1285, 792, 1289, 1298,
+        769, 397, 1302, 770, 1411, 143, 772, 780, 1286, 1413, 1291, 1426, 1299, 781, 1430, 783, 1301, 1931, 1294, 1303,
+        1287, 1280, 1290, 1429, 1296, 1297, 1422, 1300, 1431, 1927, 1304, 1920, 1428, 1292, 1293,
+    ),
+    (
+        514, 266, 269, 3, 4, 518, 5, 7, 11, 14, 15, 524, 394, 1536, 397, 640, 1664, 1800, 1801, 1811,
+        131, 132, 133, 135, 528, 641, 18, 139, 142, 657, 143, 909, 899, 128, 146, 385, 1032, 1033, 145, 1024,
+        1043, 1034, 1025, 1160, 1028, 1161, 1155, 1029, 1041, 1031, 1165, 1035, 1038, 1152, 1171, 1162, 1153, 1039, 1156, 1026,
+        1157, 1042, 1169, 1030, 1159, 1036, 1040, 1163, 1166, 1167, 1154, 1170, 1158, 1422, 1164, 1168, 1410,
+    ),
+    (
+        512, 513, 262, 267, 277, 7, 1536, 648, 1664, 1795, 1797, 1801, 1810, 1814, 390, 395, 514, 405, 516, 654,
+        524, 659, 135, 136, 525, 663, 1027, 527, 10, 16, 403, 17, 1029, 1033, 1042, 1046, 20, 24, 1155, 142,
+        1032, 1030, 138, 1035, 407, 144, 1043, 145, 1157, 148, 1045, 1161, 1170, 1038, 1174, 1160, 1158, 152, 1047, 1163,
+        1031, 1171, 1024, 1173, 1034, 1040, 1166, 1041, 1175, 1044, 1931, 1048, 1159, 1025, 1152, 1026, 1028, 1162, 1036, 1168,
+        1169, 1037, 1172, 1927, 1039, 1920, 1176, 1153, 1154, 1156, 1164, 1165, 1167, 1409, 1410, 1412, 1943,
+    ),
+)
+
+
+def lanes(n):
+    return -(-n // 128) * 128
+
+
+def lent(shard):
+    return shard // UNITS * sum(parts for parts, _, _, moved in CUTS[1] if moved)
+
+
+def fetched(shard, core):
+    return lanes(shard // UNITS * sum(parts for parts, color, _, _ in CUTS[core] if color == 2))
+
+
+def cut(shard, ushard, core):
+    table, unit, room = CUTS[core], shard // UNITS, lanes(lent(shard))
     places, off = {}, 0
-    for i in sorted(range(len(CUTS)), key=lambda i: CUTS[i][1] != 2):
+    for i in sorted(range(len(table)), key=lambda i: (table[i][3], table[i][1] != 2)):
+        if table[i][3] and off < shard + room - lent(shard):
+            off = shard + room - lent(shard)
         places[i] = off
-        off += CUTS[i][0] * unit
+        off += table[i][0] * unit
     return [
-        (places[i], parts * unit, color, mode) if parts else (shard, ushard, color, mode)
-        for i, (parts, color, mode) in enumerate(CUTS)
+        (places[i], parts * unit, color, mode, moved) if parts else (shard + room, ushard, color, mode, moved)
+        for i, (parts, color, mode, moved) in enumerate(table)
     ]
 
 
-def fetched(pieces):
-    return sum(n for _, n, color, _ in pieces if color == 2)
-
-
 def working(color):
-    return {3: ("inner",), 5: ("inner",), 4: ("outer",), 6: ("outer",)}.get(color, ROLES)
+    return {3: ("inner",), 5: ("inner",), 4: ("outer",), 6: ("outer",)}.get(color, ("outer", "inner"))
 
 
 def direct(color, mode):
@@ -155,7 +204,7 @@
 
 def landing(pieces):
     slots = {}
-    for i, (_, _, color, mode) in enumerate(pieces):
+    for i, (_, _, color, mode, moved) in enumerate(pieces):
         for kind in (Y, X, ZI, ZM):
             slots[kind, i] = len(slots)
         if color >= 3:
@@ -168,115 +217,11 @@
             slots[B, i] = slots[ZM, i]
         if direct(color, mode):
             slots[ZF, i] = len(slots)
+        if moved:
+            for kind, modes in ((ZO, (1, 3)), (B, (0, 3)), (F, (1, 2, 3))):
+                if mode in modes:
+                    slots[kind, i] = len(slots)
     return slots
-
-
-def plan(pieces):
-    free, links, arrive = {}, {}, {}
-    out = {role: [] for role in ROLES}
-    todo = {role: [] for role in ROLES}
-    starts = {role: {"y_send": [], "x_first": [], "z_first": []} for role in ROLES}
-    early = any(color == 2 for _, _, color, _ in pieces)
-    for i, (_, _, color, mode) in enumerate(pieces):
-        first_x = color in (1, 5, 6)
-        landed = Y if first_x else X
-        for role in working(color):
-            if color == 2:
-                arrive[role, "P", i] = EARLY
-                todo[role].append(("p_send", i, ("P",)))
-                continue
-            if color >= 3:
-                todo[role].append(("z_join", i, (ZL,)))
-                starts["outer" if role == "inner" else "inner"]["z_first"].append(i)
-            else:
-                starts[role]["x_first" if first_x else "y_send"].append(i)
-            todo[role].append(("y_second", i, (X,)) if first_x else ("x_send", i, (Y,)))
-        if "outer" in working(color):
-            todo["outer"].append(("z_in", i, (landed,)))
-        needs = (landed,) * ("inner" in working(color)) + (ZI,) * ("outer" in working(color))
-        if direct(color, mode):
-            todo["inner"] += [("z_own", i, (landed,)), ("z_out", i, (ZI, ZM, ZF))]
-        else:
-            todo["inner"] += [("z_mid", i, needs), ("z_out", i, (ZM,))]
-        if mode in (0, 2):
-            todo["outer"].append(("relay", i, (ZO,)))
-        if mode in (1, 2):
-            todo["inner" if mode == 1 else "outer"].append(("forward", i, (B,)))
-    if early:
-        for role in ROLES:
-            links[role, Y] = 128 / RATE
-            arrive[role, "L", 0] = EARLY - 1.1
-            arrive[role, "G", 0] = EARLY - 0.1
-            todo[role] += [("p_low", 0, ("L",)), ("p_get", 0, ("G",))]
-
-    def move(role, link, rows, now, to, kind, i, then=None):
-        begin = max(now, links.get((role, link), 0.0))
-        done = begin + rows / RATE
-        links[role, link] = done
-        if then:
-            begin = max(begin + MORE, links.get(then, 0.0))
-            done = max(begin + rows / RATE, done + MORE)
-            links[then] = done
-        arrive[to, kind, i] = max(done + HOP, arrive.get((to, kind, i), 0.0))
-
-    def carry(role, op, i, now):
-        _, n, color, mode = pieces[i]
-        h = n // 2
-        first_x = color in (1, 5, 6)
-        if op == "z_first":
-            move(role, ZI if role == "outer" else ZO, 2 * n, now, "inner" if role == "outer" else "outer", ZL, i)
-        elif op == "y_send" or (op == "z_join" and not first_x):
-            move(role, Y, n, now, role, Y, i)
-        elif op in ("x_send", "p_send"):
-            move(role, X, h, now, role, X, i)
-        elif op == "x_first" or op == "z_join":
-            move(role, X, n, now, role, X, i)
-        elif op == "y_second":
-            move(role, Y, h, now, role, Y, i)
-        elif op == "z_in":
-            move(role, ZI, h, now, "inner", ZI, i)
-            if direct(color, mode):
-                move(role, ZI, h, now, "inner", ZF, i, ("inner", ZM))
-        elif op in ("z_mid", "z_own"):
-            move(role, ZM, h, now, role, ZM, i)
-        elif op == "z_out":
-            if mode == 3:
-                move(role, X, h, now, "outer", F, i, (role, ZO))
-            if mode != 2:
-                move(role, X, h, now, role, B, i)
-            move(role, ZO, h, now, "outer", ZO, i)
-        elif op == "relay":
-            move(role, X, h, now, role, B, i)
-        elif op == "forward":
-            to = "outer" if role == "inner" else "inner"
-            move(role, ZO if role == "inner" else ZI, h, now, to, F, i)
-
-    while True:
-        options = []
-        for role in ROLES:
-            clock = free.get(role, 0.0)
-            for op, i, kinds in todo[role]:
-                if all((role, kind, i) in arrive for kind in kinds):
-                    ready = max(arrive[role, kind, i] for kind in kinds)
-                    options.append((max(clock, ready), ready, role, op, i, kinds))
-            side = ZI if role == "outer" else ZO
-            for op, link, deep in (("y_send", Y, DEEP[0]), ("x_first", X, DEEP[1]), ("z_first", side, DEEP[2])):
-                if starts[role][op]:
-                    ready = links.get((role, link), 0.0) - deep
-                    options.append((max(clock, ready), ready, role, op, starts[role][op][0], None))
-        if not options:
-            return out
-        now, _, role, op, i, kinds = min(options, key=lambda option: option[:2])
-        if kinds is None:
-            starts[role][op].pop(0)
-        else:
-            todo[role].remove((op, i, kinds))
-        out[role].append((now, op, i))
-        now += COST.get(op, 0.03)
-        free[role] = now
-        carry(role, op, i, now)
-        out["end"] = max(arrive.values())
-        out["links"] = links
 
 
 def fits(seq_count, dp_count):
@@ -292,10 +237,10 @@
     x_hbm, w_hbm, u_hbm, q_hbm, k_hbm, v_hbm, g_hbm,
     qo_ref, ko_ref, vo_ref, down_ref, up_ref,
     x_ref, w_ref, u_ref, four_ref, xs_ref, xr_ref, xt_ref,
-    st_ref, pair_ref, kvr_ref, qgr_ref, ox_ref, sxs_ref, sxr_ref,
+    st_ref, pair_ref, kvr_ref, qgr_ref, ox_ref, sxs_ref, sxr_ref, lead_ref,
     ls_ref, lr_ref, ups_ref, upr_ref, fg_ref,
     ys_ref, yr_ref, acc_ref, xrs_ref, zs_ref, zr_ref, zm_ref, zf_ref, zl_ref,
-    ps_ref, pr_ref, pt_ref, lo_ref, them_ref, pre_s, pre_r,
+    ps_ref, pr_ref, pt_ref, lo_ref, them_ref, xes_ref, xer_ref, lent_ref, pre_s, pre_r,
     load_sem, core_s, core_r, scan_s, scan_r, sx_s, sx_r,
     send_s, hop_r,
 ):
@@ -331,8 +276,10 @@
     rows, width = qo_ref.shape
     shard = down_ref.shape[0]
     ushard = up_ref.shape[0]
-    pieces = cut(shard, ushard)
-    early = fetched(pieces)
+    early = [fetched(shard, core) for core in range(CORES)]
+    moved_rows = lent(shard)
+    room = lanes(moved_rows)
+    base = shard + room
     pltpu.make_async_copy(four_ref, four_ref, load_sem.at[2]).wait()
     q, k, v, g = four_ref[0], four_ref[1], four_ref[2], four_ref[3]
     st_ref[0] = dot(k, v, 0, 0)
@@ -361,30 +308,32 @@
             pl.when(z >= d)(downs[d - 1].start)
         return ups, downs
 
-    def collect(ups, downs, part):
-        sxs_ref[:, part, :] = jnp.zeros((2, lead, width), jnp.float32)
+    def collect(scans, part, which):
+        sxs_ref[which, part, :] = jnp.zeros((lead, width), jnp.float32)
         for d in range(1, depth):
-            @pl.when(z >= d)
+            @pl.when(z + d < depth if which else z >= d)
             def _(d=d):
-                ups[d - 1].wait_recv()
-                sxs_ref[0, part, :] += kvr_ref[d - 1, part, :]
-
-            @pl.when(z + d < depth)
-            def _(d=d):
-                downs[d - 1].wait_recv()
-                sxs_ref[1, part, :] += qgr_ref[d - 1, part, :]
+                scans[which][d - 1].wait_recv()
+                sxs_ref[which, part, :] += (kvr_ref, qgr_ref)[which][d - 1, part, :]
 
     scan_a = scan(st_ref, first, 0)
 
     load_x.wait()
     core_copies, extra = [], []
-    if early:
-        for at, where, core in ((0, across, c), (1, apart, 1 - c)):
-            cols = pl.ds(pl.multiple_of(((1 - y) * CORES + core) * shard, 128), early)
-            ps_ref[at] = x_ref[:, cols].astype(jnp.float32)
-            copy = remote(ps_ref.at[at], pr_ref.at[at], pre_s.at[at], pre_r.at[at], where)
+    for core in range(CORES):
+        if early[core]:
+            cols = pl.ds(pl.multiple_of(((1 - y) * CORES + core) * shard, 128), early[core])
+            mine = ps_ref.at[core, :, 0 : early[core]]
+            mine[...] = x_ref[:, cols].astype(jnp.float32)
+            where = {"seq": seq, "dp": (1 - y) * CORES + core}
+            copy = remote(mine, pr_ref.at[c, :, 0 : early[core]], pre_s.at[core], pre_r.at[c], where)
             copy.start()
             extra.append(copy)
+    if room:
+        for part in range(2):
+            xes_ref[part] = x_ref[:, (part * CORES + 1) * shard - room : (part * CORES + 1) * shard].astype(jnp.float32)
+        lend = remote(xes_ref, xer_ref, pre_s.at[4], pre_r.at[4], mate)
+        pl.when(c == 0)(lend.start)
     for part in range(2):
         cols = pl.ds(pl.multiple_of((part * CORES + 1 - c) * shard, 128), shard)
         xs_ref[part] = x_ref[:, cols].astype(jnp.float32)
@@ -407,30 +356,46 @@
 
     for part in range(2):
         cols = pl.ds(pl.multiple_of((part * CORES + c) * shard, 128), shard)
-        xt_ref[part, :, 0:rows] = x_ref[:, cols].T
+        xt_ref[part, 0:shard, 0:rows] = x_ref[:, cols].T
 
     load_w.wait()
     low = jnp.dot(x_ref[...], w_ref[...], preferred_element_type=jnp.float32).astype(jnp.bfloat16)
 
-    collect(*scan_a, first)
-    lead_sum = sxs_ref[:, first, :]
-
-    @pl.when(x == 0)
-    def _():
-        sxs_ref[0, first, :] += st_ref[0, first, :]
-
-    @pl.when(x == 1)
-    def _():
-        sxs_ref[1, first, :] += st_ref[1, first, :]
-
-    swap = remote(sxs_ref.at[:, first, :], sxr_ref, sx_s.at[0], sx_r.at[0], beside)
-    swap.start()
+    swaps = [
+        remote(sxs_ref.at[which, first, :], sxr_ref.at[which], sx_s.at[2 * which], sx_r.at[2 * which], beside)
+        for which in range(2)
+    ]
+
+    def settle(which):
+        collect(scan_a, first, which)
+        lead_ref[which] = sxs_ref[which, first, :]
+
+        @pl.when(x == which)
+        def _():
+            sxs_ref[which, first, :] += st_ref[which, first, :]
+
+        swaps[which].start()
+
+    for here, turns in ((z < depth // 2, (0, 1)), (z >= depth // 2, (1, 0))):
+        @pl.when(here)
+        def _(turns=turns):
+            for which in turns:
+                settle(which)
 
     for part in range(2):
         core_copies[part].wait_recv()
-        xt_ref[part, :, rows:] = xr_ref[part].astype(jnp.bfloat16).T
-
-    collect(*scan_b, second)
+        xt_ref[part, 0:shard, rows:] = xr_ref[part].astype(jnp.bfloat16).T
+
+    if room:
+        @pl.when(c == 1)
+        def _():
+            lend.wait_recv()
+            for part in range(2):
+                xt_ref[part, shard:base, 0:rows] = x_ref[:, (part * CORES + 1) * shard - room : (part * CORES + 1) * shard].T
+                xt_ref[part, shard:base, rows:] = xer_ref[part].astype(jnp.bfloat16).T
+
+    for which in range(2):
+        collect(scan_b, second, which)
 
     @pl.when(x == 1)
     def _():
@@ -440,8 +405,9 @@
     def _():
         sxs_ref[1, second, :] += ox_ref[1]
 
-    swap.wait_recv()
-    states = jnp.concatenate([lead_sum + sxr_ref[...], sxs_ref[:, second, :]], axis=1).astype(jnp.bfloat16)
+    for swap in swaps:
+        swap.wait_recv()
+    states = jnp.concatenate([lead_ref[...] + sxr_ref[...], sxs_ref[:, second, :]], axis=1).astype(jnp.bfloat16)
     prefix, suffix = states[0], states[1]
     q_grad = (factor * (q_in + dot(g, prefix, 1, 1))).astype(jnp.bfloat16)
     k_grad = (factor * (k_in + dot(v, suffix, 1, 1))).astype(jnp.bfloat16)
@@ -452,11 +418,11 @@
     ls_ref[...] = low_grad.astype(jnp.float32)
     low_copy = remote(ls_ref, lr_ref, core_s.at[2], core_r.at[2], mate)
     low_copy.start()
-    if early:
-        low_across = remote(ls_ref, lo_ref.at[0], pre_s.at[2], pre_r.at[2], across)
+    if sum(early):
+        low_across = remote(ls_ref, lo_ref.at[c], pre_s.at[2], pre_r.at[2], across)
         low_across.start()
-        low_apart = remote(lo_ref.at[0], lo_ref.at[1], pre_s.at[3], pre_r.at[3], mate)
-        extra.extend([low_across, low_apart])
+        low_apart = remote(lo_ref.at[c], lo_ref.at[c], pre_s.at[3], pre_r.at[3], mate)
+        extra.append(low_across)
     qo_ref[...] = q_grad
     ko_ref[...] = k_grad
     vo_ref[...] = v_grad
@@ -471,12 +437,15 @@
     inward, outward, opposite = along(mid), along(end), along(depth - 1 - z)
     further = along(depth - 1 - mid)
     corner = {"seq": end * 2 + (1 - x), "dp": dp}
-    slots = landing(pieces)
+    cuts = [cut(shard, ushard, core) for core in range(CORES)]
+    landings = [landing(pieces) for pieces in cuts]
+    last = max(len(slots) for slots in landings)
     sent = {}
+    pieces, slots = [], {}
 
     def send(role, kind, i, src, dst, where):
         sent[kind] = sent.get(kind, 0) + src.shape[0]
-        at = slots.get((kind, i), len(slots))
+        at = slots.get((kind, i), last)
         remote(src, dst, send_s.at[kind], hop_r.at[at], where).start()
 
     def arrived(kind, i, like):
@@ -484,7 +453,7 @@
 
     def partial(i, part):
         off, n = pieces[i][:2]
-        if off < shard:
+        if off < base:
             return jnp.dot(xt_ref[part, off : off + n, :], both, preferred_element_type=jnp.float32)
         mine = pl.ds(pl.multiple_of((part * CORES + c) * ushard, 8), ushard)
         return fg_ref[mine, :] + upr_ref[part]
@@ -499,11 +468,19 @@
 
     def place(i, which):
         off, n = pieces[i][:2]
-        ref, base = (down_ref, off) if off < shard else (up_ref, 0)
-        return ref.at[pl.ds(pl.multiple_of(base + which * (n // 2), 8), n // 2), :]
-
-    def perform(role, op, i):
-        off, n, color, mode = pieces[i]
+        ref, start = (up_ref, 0) if off >= base else (lent_ref, off - shard) if off >= shard else (down_ref, off)
+        return ref.at[pl.ds(pl.multiple_of(start + which * (n // 2), 8), n // 2), :]
+
+    def deliver(role, i, which):
+        off, n, _, _, moved = pieces[i]
+        if moved:
+            h = n // 2
+            home = down_ref.at[pl.ds(pl.multiple_of(off - room + which * h, 8), h), :]
+            sent[D] = sent.get(D, 0) + h
+            remote(place(i, which), home, send_s.at[D], hop_r.at[last + 1], mate).start()
+
+    def perform(role, core, op, i):
+        off, n, color, mode, moved = pieces[i]
         h = n // 2
         first_x = color in (1, 5, 6)
         workers = working(color)
@@ -511,7 +488,7 @@
         small = short(i)
         landed = Y if first_x else X
         if op == "y_send":
-            if off >= shard:
+            if off >= base:
                 up_copy.wait_recv()
             ys_ref[whole, :] = partial(i, 1 - y)
             send(role, Y, i, ys_ref.at[whole, :], yr_ref.at[whole, :], across)
@@ -532,12 +509,14 @@
                 send(role, Y, i, ys_ref.at[whole, :], yr_ref.at[whole, :], across)
         elif op == "p_low":
             low_across.wait_recv()
-            low_apart.start()
+            if early[1 - core]:
+                low_apart.start()
         elif op == "p_get":
-            low_apart.wait_recv()
+            remote(ls_ref, ls_ref, pre_s.at[3], pre_r.at[3], mate).wait_recv()
             for at in range(2):
-                extra[at].wait_recv()
-                pt_ref[:, at * rows : (at + 1) * rows] = pr_ref[at].astype(jnp.bfloat16).T
+                theirs = pr_ref.at[at, :, 0 : early[core]]
+                remote(theirs, theirs, pre_s.at[at], pre_r.at[at], mate).wait_recv()
+                pt_ref[0 : early[core], at * rows : (at + 1) * rows] = theirs[...].astype(jnp.bfloat16).T
                 them_ref[at * rows : (at + 1) * rows, :] = lo_ref[at].astype(jnp.bfloat16)
         elif op == "p_send":
             acc_ref[whole, :] = partial(i, y) + jnp.dot(
@@ -597,14 +576,23 @@
             if mode in (0, 1, 3):
                 send(role, B, i, spot, spot, beside)
             send(role, ZO, i, spot, spot, outward)
+            deliver(role, i, x)
         elif op == "relay":
             spot = place(i, x)
             arrived(ZO, i, spot)
             send(role, B, i, spot, spot, beside)
+            deliver(role, i, x)
         elif op == "forward":
             spot = place(i, 1 - x)
             arrived(B, i, spot)
             send(role, F, i, spot, spot, outward if role == "inner" else inward)
+            deliver(role, i, 1 - x)
+        elif op == "near":
+            arrived(ZO, i, place(i, x))
+            deliver(role, i, x)
+        elif op == "far":
+            arrived(B if mode == 0 or (mode == 3 and role == "inner") else F, i, place(i, 1 - x))
+            deliver(role, i, 1 - x)
 
     up_all = dot(fg, low, 0, 0)
     fg_ref[...] = up_all
@@ -615,21 +603,34 @@
     up_copy.start()
 
     for role, here in (("outer", outer), ("inner", inner)):
-        @pl.when(here)
-        def _(role=role):
-            sent.clear()
-            for _, op, i in plan(pieces)[role]:
-                perform(role, op, i)
-            late = sum(n // 2 for _, n, _, mode in pieces if mode in (1, 3) and role == "outer") + sum(
-                n // 2 for _, n, _, mode in pieces if (role, mode) not in (("outer", 2), ("inner", 1)))
-            like = ys_ref.at[0:late, :]
-            remote(like, like, send_s.at[0], hop_r.at[len(slots)], mate).wait_recv()
-            for kind, rows in list(sent.items()):
-                like = zl_ref.at[:, 0 : rows // 2, :] if kind == ZL else ys_ref.at[0:rows, :]
-                remote(like, like, send_s.at[kind], hop_r.at[len(slots)], mate).wait_send()
+        for core in range(CORES):
+            @pl.when(here & (c == core))
+            def _(role=role, core=core):
+                sent.clear()
+                slots.clear()
+                slots.update(landings[core])
+                pieces[:] = cuts[core]
+                for code in ORDERS[2 * (role == "inner") + core]:
+                    perform(role, core, OPS[code // UNITS], code % UNITS)
+                late = 0
+                for _, n, _, mode, moved in pieces:
+                    if not moved:
+                        late += n // 2 * (mode in (1, 3) and role == "outer")
+                        late += n // 2 * ((role, mode) not in (("outer", 2), ("inner", 1)))
+                for rows_in, at in ((late, last), ((1 - core) * moved_rows, last + 1)):
+                    if rows_in:
+                        like = ys_ref.at[0:rows_in, :]
+                        remote(like, like, send_s.at[0], hop_r.at[at], mate).wait_recv()
+                for kind, rows_out in list(sent.items()):
+                    like = zl_ref.at[:, 0 : rows_out // 2, :] if kind == ZL else ys_ref.at[0:rows_out, :]
+                    remote(like, like, send_s.at[kind], hop_r.at[last], mate).wait_send()
+                if early[1 - core]:
+                    low_apart.wait_send()
+                if room and core == 0:
+                    lend.wait_send()
 
     remote(kvr_ref, kvr_ref, scan_s.at[0], scan_r.at[0], mate).wait_send()
-    for copy in core_copies + [other, swap, low_copy, up_copy] + extra:
+    for copy in core_copies + swaps + [other, low_copy, up_copy] + extra:
         copy.wait_send()
 
 
@@ -653,9 +654,11 @@
     inverse = 1.0 / math.sqrt(length * dp_count)
     depth = seq_count // 2
     shard, ushard = model // dp_count, features // dp_count
-    total = shard + ushard
-    pieces = cut(shard, ushard)
-    early = max(fetched(pieces), rows)
+    room = lanes(lent(shard))
+    total = shard + room + ushard
+    slots = max(len(landing(cut(shard, ushard, core))) for core in range(CORES))
+    early = max([fetched(shard, core) for core in range(CORES)] + [128])
+    spare = max(room, 128)
     f32, bf16 = jnp.float32, jnp.bfloat16
     dma = pltpu.SemaphoreType.DMA
     vmem = pl.BlockSpec(memory_space=pltpu.VMEM)
@@ -676,13 +679,14 @@
             pltpu.VMEM((4, rows, width), bf16),
             pltpu.VMEM((2, rows, shard), f32),
             pltpu.VMEM((2, rows, shard), f32),
-            pltpu.VMEM((2, shard, 2 * rows), bf16),
+            pltpu.VMEM((2, shard + room, 2 * rows), bf16),
             pltpu.VMEM((2, width, width), f32),
             pltpu.VMEM((2, width, width), f32),
             pltpu.VMEM((depth - 1, width, width), f32),
             pltpu.VMEM((depth - 1, width, width), f32),
             pltpu.VMEM((2, width // 2, width), f32),
             pltpu.VMEM((2, width, width), f32),
+            pltpu.VMEM((2, width // 2, width), f32),
             pltpu.VMEM((2, width // 2, width), f32),
             pltpu.VMEM((rows, rank), f32),
             pltpu.VMEM((rows, rank), f32),
@@ -703,11 +707,14 @@
             pltpu.VMEM((early, 2 * rows), bf16),
             pltpu.VMEM((2, rows, rank), f32),
             pltpu.VMEM((2 * rows, rank), bf16),
-            dma((4,)), dma((4,)),
+            pltpu.VMEM((2, rows, spare), f32),
+            pltpu.VMEM((2, rows, spare), f32),
+            pltpu.VMEM((spare, rank), f32),
+            dma((5,)), dma((5,)),
             dma((4,)), dma((4,)), dma((4,)),
             dma((1,)), dma((2 * depth - 2,)),
-            dma((2,)), dma((2,)),
-            dma((KINDS,)), dma((len(landing(pieces)) + 1,)),
+            dma((3,)), dma((3,)),
+            dma((KINDS,)), dma((slots + 2,)),
         ],
         compiler_params=pltpu.CompilerParams(
             collective_id=0, has_side_effects=True

time: 50.2 us -> 48.4 us (0.964)
  the two profiles are of different devices: /device:TPU:0 before, /device:TPU:1 now
where the time goes in v4:
time: 48.4 us; the launch traced here: 48.2 us
  Pallas kernels  47.6 us (98%)
  between operations  0.64 us (1%)
    pallas_call x1, Pallas kernels, fast(): pl.pallas_call(functools.partial(fused_kernel, depth, factor, inverse), o...  46.5 us
    pallas_call x1, Pallas kernels, fast(): pl.pallas_call(write_out, out_shape=shapes, in_specs=[vmem] * 5, out_spec...  1.05 us

profile of v4, /device:TPU:1, one launch (start us, length us, event | category | flops | bytes accessed | tf_op | source)
XLA Modules:
  0.0 48.2 jit_solution(288000937879769625)
XLA Ops:
  0.6 46.5 %shard_map.110 = (bf16[128,128]{1,0:T(8,128)(2,1)S(1)}, bf16[128,128]{1,0:T(8,128)(2,1)S(1)}, bf16[128,128]{1,0:T(8,128)(2,1)S(1)}, f32[2048,128]{1,0:T(8,128)S(1)}, f32[96,128]{1,0:T(8,128)S(1)}) custom-call(bf16[128,8192]{1,0:T(8,128)(2,1)} %bitcast.8, bf16[8192,128]{1,0:T(8,128)(2,1)} %w_hbm.1, bf16[384,128]{1,0:T(8,128)(2,1)} %u_hbm.1, ...), custom_call_target="tpu_custom_call" | custom-call | tf_op jit(solution)/shard_map/pallas_call | solution.py:670
  47.2 1.1 %shard_map.111 = (bf16[128,128]{1,0:T(8,128)(2,1)}, bf16[128,128]{1,0:T(8,128)(2,1)}, bf16[128,128]{1,0:T(8,128)(2,1)}, f32[2048,128]{1,0:T(8,128)}, f32[96,128]{1,0:T(8,128)}) custom-call(bf16[128,128]{1,0:T(8,128)(2,1)S(1)} %get-tuple-element.15.refs_0_, bf16[128,128]{1,0:T(8,128)(2,1)S(1)} %get-tuple-element.16.refs_1_, ...), custom_call_target="tpu_custom_call" | custom-call | tf_op jit(solution)/shard_map/pallas_call | solution.py:727

commit v5 on v4

--- a/solution.py
+++ b/solution.py
@@ -202,26 +202,38 @@
     return mode == 3 and color < 3
 
 
+def waits(role, color, mode, moved):
+    work = role in working(color)
+    kinds = [Y] * (work and color != 2) + [X] * work + [ZL] * (work and color >= 3)
+    if role == "inner":
+        kinds += [ZM] + [ZI] * ("outer" in working(color)) + [ZF] * direct(color, mode)
+        kinds += [B] * (mode == 1 or (moved and mode in (0, 3))) + [F] * (moved and mode == 2)
+    else:
+        kinds += [ZO] * (mode in (0, 2) or moved)
+        kinds += [B] * (mode == 2 or (moved and mode == 0)) + [F] * (moved and mode in (1, 3))
+    return kinds
+
+
 def landing(pieces):
     slots = {}
-    for i, (_, _, color, mode, moved) in enumerate(pieces):
-        for kind in (Y, X, ZI, ZM):
-            slots[kind, i] = len(slots)
-        if color >= 3:
-            slots[ZL, i] = len(slots)
-        if mode in (0, 2):
-            slots[ZO, i] = slots[ZI, i]
-        if mode == 1:
-            slots[B, i] = len(slots)
-        if mode == 2:
-            slots[B, i] = slots[ZM, i]
-        if direct(color, mode):
-            slots[ZF, i] = len(slots)
-        if moved:
-            for kind, modes in ((ZO, (1, 3)), (B, (0, 3)), (F, (1, 2, 3))):
-                if mode in modes:
-                    slots[kind, i] = len(slots)
+    for role in ("outer", "inner"):
+        spots = [
+            (role, kind, i)
+            for i, (_, _, color, mode, moved) in enumerate(pieces)
+            for kind in waits(role, color, mode, moved)
+        ]
+        slots.update((spot, at) for at, spot in enumerate(spots))
     return slots
+
+
+def reached(role, kind):
+    if kind in (ZI, ZF):
+        return "inner"
+    if kind == ZO:
+        return "outer"
+    if kind in (F, ZL):
+        return "outer" if role == "inner" else "inner"
+    return role
 
 
 def fits(seq_count, dp_count):
@@ -294,7 +306,6 @@
     lead = width // 2
     first, second = slice(0, lead), slice(lead, width)
     other = remote(st_ref.at[:, second, :], ox_ref, sx_s.at[1], sx_r.at[1], beside)
-    other.start()
 
     def scan(source, part, at):
         ups, downs = [], []
@@ -303,10 +314,12 @@
             back = at * (depth - 1) + depth - d - 1
             ups.append(remote(source.at[0, part, :], kvr_ref.at[d - 1, part, :], scan_s.at[0], scan_r.at[slot], along(lax.rem(z + d, depth))))
             downs.append(remote(source.at[1, part, :], qgr_ref.at[d - 1, part, :], scan_s.at[0], scan_r.at[back], along(lax.rem(z - d + depth, depth))))
-        for d in range(1, depth):
-            pl.when(z + d < depth)(ups[d - 1].start)
-            pl.when(z >= d)(downs[d - 1].start)
         return ups, downs
+
+    def launch(scans):
+        for d in reversed(range(1, depth)):
+            pl.when(z + d < depth)(scans[0][d - 1].start)
+            pl.when(z >= d)(scans[1][d - 1].start)
 
     def collect(scans, part, which):
         sxs_ref[which, part, :] = jnp.zeros((lead, width), jnp.float32)
@@ -318,6 +331,11 @@
 
     scan_a = scan(st_ref, first, 0)
 
+    def begin():
+        other.start()
+        launch(scan_a)
+
+    pl.when(c == 0)(begin)
     load_x.wait()
     core_copies, extra = [], []
     for core in range(CORES):
@@ -341,10 +359,6 @@
         copy.start()
         core_copies.append(copy)
 
-    other.wait_recv()
-    pair_ref[:, second, :] = st_ref[:, second, :] + ox_ref[...]
-    scan_b = scan(pair_ref, second, 1)
-
     r_idx = lax.broadcasted_iota(jnp.int32, (rows, rows), 0)
     c_idx = lax.broadcasted_iota(jnp.int32, (rows, rows), 1)
     causal = r_idx >= c_idx
@@ -358,8 +372,14 @@
         cols = pl.ds(pl.multiple_of((part * CORES + c) * shard, 128), shard)
         xt_ref[part, 0:shard, 0:rows] = x_ref[:, cols].T
 
+    pl.when(c == 1)(begin)
     load_w.wait()
     low = jnp.dot(x_ref[...], w_ref[...], preferred_element_type=jnp.float32).astype(jnp.bfloat16)
+
+    other.wait_recv()
+    pair_ref[:, second, :] = st_ref[:, second, :] + ox_ref[...]
+    scan_b = scan(pair_ref, second, 1)
+    launch(scan_b)
 
     swaps = [
         remote(sxs_ref.at[which, first, :], sxr_ref.at[which], sx_s.at[2 * which], sx_r.at[2 * which], beside)
@@ -439,17 +459,17 @@
     corner = {"seq": end * 2 + (1 - x), "dp": dp}
     cuts = [cut(shard, ushard, core) for core in range(CORES)]
     landings = [landing(pieces) for pieces in cuts]
-    last = max(len(slots) for slots in landings)
+    last = 1 + max(at for slots in landings for at in slots.values())
     sent = {}
     pieces, slots = [], {}
 
     def send(role, kind, i, src, dst, where):
         sent[kind] = sent.get(kind, 0) + src.shape[0]
-        at = slots.get((kind, i), last)
+        at = slots.get((reached(role, kind), kind, i), last)
         remote(src, dst, send_s.at[kind], hop_r.at[at], where).start()
 
-    def arrived(kind, i, like):
-        remote(like, like, send_s.at[kind], hop_r.at[slots[kind, i]], mate).wait_recv()
+    def arrived(role, kind, i, like):
+        remote(like, like, send_s.at[kind], hop_r.at[slots[role, kind, i]], mate).wait_recv()
 
     def partial(i, part):
         off, n = pieces[i][:2]
@@ -499,7 +519,7 @@
             acc_ref[whole, :] = partial(i, y)
             send(role, ZL, i, acc_ref.at[whole, :], zl_ref.at[1, whole, :], where)
         elif op == "z_join":
-            arrived(ZL, i, zl_ref.at[:, whole, :])
+            arrived(role, ZL, i, zl_ref.at[:, whole, :])
             ys_ref[whole, :] = partial(i, 1 - y) + zl_ref[0, whole, :]
             if first_x:
                 send(role, X, i, ys_ref.at[half(i, 1 - x), :], yr_ref.at[high_half, :], beside)
@@ -527,7 +547,7 @@
             own = partial(i, y)
             if color >= 3:
                 own = own + zl_ref[1, whole, :]
-            arrived(Y, i, yr_ref.at[whole, :])
+            arrived(role, Y, i, yr_ref.at[whole, :])
             acc_ref[whole, :] = own + yr_ref[whole, :]
             send(role, X, i, acc_ref.at[half(i, 1 - x), :], xrs_ref.at[small, :], beside)
         elif op == "x_first":
@@ -536,38 +556,38 @@
             acc_ref[whole, :] = partial(i, y)
             send(role, X, i, acc_ref.at[half(i, 1 - x), :], yr_ref.at[low_half, :], beside)
         elif op == "y_second":
-            arrived(X, i, yr_ref.at[whole, :])
+            arrived(role, X, i, yr_ref.at[whole, :])
             ys_ref[half(i, x), :] += yr_ref[high_half, :]
             send(role, Y, i, ys_ref.at[half(i, x), :], xrs_ref.at[small, :], across)
             acc_ref[half(i, x), :] += yr_ref[low_half, :]
         elif op == "z_in":
-            arrived(landed, i, xrs_ref.at[small, :])
+            arrived(role, landed, i, xrs_ref.at[small, :])
             zs_ref[small, :] = acc_ref[half(i, x), :] + xrs_ref[small, :]
             send(role, ZI, i, zs_ref.at[small, :], zr_ref.at[small, :], inward)
             if direct(color, mode):
                 send(role, ZF, i, zs_ref.at[small, :], zf_ref.at[small, :], further)
         elif op == "z_own":
-            arrived(landed, i, xrs_ref.at[small, :])
+            arrived(role, landed, i, xrs_ref.at[small, :])
             zs_ref[small, :] = acc_ref[half(i, x), :] + xrs_ref[small, :]
             send(role, ZM, i, zs_ref.at[small, :], zm_ref.at[small, :], opposite)
         elif op == "z_mid":
             if "inner" in workers:
-                arrived(landed, i, xrs_ref.at[small, :])
+                arrived(role, landed, i, xrs_ref.at[small, :])
                 own = acc_ref[half(i, x), :] + xrs_ref[small, :]
             if "outer" in workers:
-                arrived(ZI, i, zr_ref.at[small, :])
+                arrived(role, ZI, i, zr_ref.at[small, :])
                 own = own + zr_ref[small, :] if "inner" in workers else zr_ref[small, :]
             zs_ref[small, :] = own
             send(role, ZM, i, zs_ref.at[small, :], zm_ref.at[small, :], opposite)
         elif op == "z_out":
             own = zs_ref[small, :]
             if direct(color, mode):
-                arrived(ZI, i, zr_ref.at[small, :])
+                arrived(role, ZI, i, zr_ref.at[small, :])
                 own = own + zr_ref[small, :]
-            arrived(ZM, i, zm_ref.at[small, :])
+            arrived(role, ZM, i, zm_ref.at[small, :])
             own = own + zm_ref[small, :]
             if direct(color, mode):
-                arrived(ZF, i, zf_ref.at[small, :])
+                arrived(role, ZF, i, zf_ref.at[small, :])
                 own = own + zf_ref[small, :]
             spot = place(i, x)
             spot[...] = own * inverse
@@ -579,19 +599,19 @@
             deliver(role, i, x)
         elif op == "relay":
             spot = place(i, x)
-            arrived(ZO, i, spot)
+            arrived(role, ZO, i, spot)
             send(role, B, i, spot, spot, beside)
             deliver(role, i, x)
         elif op == "forward":
             spot = place(i, 1 - x)
-            arrived(B, i, spot)
+            arrived(role, B, i, spot)
             send(role, F, i, spot, spot, outward if role == "inner" else inward)
             deliver(role, i, 1 - x)
         elif op == "near":
-            arrived(ZO, i, place(i, x))
+            arrived(role, ZO, i, place(i, x))
             deliver(role, i, x)
         elif op == "far":
-            arrived(B if mode == 0 or (mode == 3 and role == "inner") else F, i, place(i, 1 - x))
+            arrived(role, B if mode == 0 or (mode == 3 and role == "inner") else F, i, place(i, 1 - x))
             deliver(role, i, 1 - x)
 
     up_all = dot(fg, low, 0, 0)
@@ -656,7 +676,7 @@
     shard, ushard = model // dp_count, features // dp_count
     room = lanes(lent(shard))
     total = shard + room + ushard
-    slots = max(len(landing(cut(shard, ushard, core))) for core in range(CORES))
+    slots = 1 + max(max(landing(cut(shard, ushard, core)).values()) for core in range(CORES))
     early = max([fetched(shard, core) for core in range(CORES)] + [128])
     spare = max(room, 128)
     f32, bf16 = jnp.float32, jnp.bfloat16

time: 48.4 us -> 46.6 us (0.963)
  the two profiles are of different devices: /device:TPU:1 before, /device:TPU:0 now
where the time goes in v5:
time: 46.6 us; the launch traced here: 46.5 us
  Pallas kernels  45.8 us (98%)
  between operations  0.64 us (1%)
    pallas_call x1, Pallas kernels, fast(): pl.pallas_call(functools.partial(fused_kernel, depth, factor, inverse), o...  44.8 us
    pallas_call x1, Pallas kernels, fast(): pl.pallas_call(write_out, out_shape=shapes, in_specs=[vmem] * 5, out_spec...  1.05 us

profile of v5, /device:TPU:0, one launch (start us, length us, event | category | flops | bytes accessed | tf_op | source)
XLA Modules:
  0.0 46.5 jit_solution(2863016627783137066)
XLA Ops:
  0.6 44.8 %shard_map.110 = (bf16[128,128]{1,0:T(8,128)(2,1)S(1)}, bf16[128,128]{1,0:T(8,128)(2,1)S(1)}, bf16[128,128]{1,0:T(8,128)(2,1)S(1)}, f32[2048,128]{1,0:T(8,128)S(1)}, f32[96,128]{1,0:T(8,128)S(1)}) custom-call(bf16[128,8192]{1,0:T(8,128)(2,1)} %bitcast.8, bf16[8192,128]{1,0:T(8,128)(2,1)} %w_hbm.1, bf16[384,128]{1,0:T(8,128)(2,1)} %u_hbm.1, ...), custom_call_target="tpu_custom_call" | custom-call | tf_op jit(solution)/shard_map/pallas_call | solution.py:690
  45.4 1.1 %shard_map.111 = (bf16[128,128]{1,0:T(8,128)(2,1)}, bf16[128,128]{1,0:T(8,128)(2,1)}, bf16[128,128]{1,0:T(8,128)(2,1)}, f32[2048,128]{1,0:T(8,128)}, f32[96,128]{1,0:T(8,128)}) custom-call(bf16[128,128]{1,0:T(8,128)(2,1)S(1)} %get-tuple-element.15.refs_0_, bf16[128,128]{1,0:T(8,128)(2,1)S(1)} %get-tuple-element.16.refs_1_, ...), custom_call_target="tpu_custom_call" | custom-call | tf_op jit(solution)/shard_map/pallas_call | solution.py:747

commit v6 on v5

--- a/solution.py
+++ b/solution.py
@@ -140,30 +140,30 @@
 )
 ORDERS = (
     (
-        512, 266, 513, 269, 3, 4, 5, 7, 11, 529, 14, 15, 394, 1536, 397, 642, 1664, 1800, 1801, 1811,
-        131, 132, 133, 135, 18, 139, 646, 142, 776, 777, 652, 143, 787, 778, 771, 781, 772, 773, 656, 775,
-        130, 779, 146, 390, 782, 396, 144, 783, 770, 786, 774, 780, 784, 1288, 1289, 1280, 1299, 1290, 1281, 1284,
-        1285, 1297, 1287, 1291, 1409, 1412, 1413, 1295, 1298, 1286, 1292, 1296,
+        512, 266, 513, 269, 3, 4, 5, 7, 11, 529, 14, 15, 1536, 394, 397, 642, 1664, 1800, 1801, 1811,
+        131, 132, 133, 135, 18, 139, 646, 142, 776, 777, 652, 143, 778, 787, 771, 781, 772, 773, 656, 775,
+        130, 779, 146, 390, 782, 396, 144, 783, 770, 786, 774, 780, 784, 1288, 1289, 1290, 1280, 1299, 1281, 1284,
+        1285, 1287, 1297, 1291, 1409, 1412, 1413, 1295, 1298, 1286, 1292, 1296,
     ),
     (
         520, 526, 531, 535, 262, 267, 277, 7, 1536, 1664, 1795, 1797, 1801, 1810, 1814, 390, 395, 405, 771, 640,
-        773, 135, 777, 10, 786, 790, 16, 774, 17, 779, 20, 24, 789, 641, 384, 138, 144, 642, 145, 148,
-        644, 775, 652, 152, 653, 768, 385, 778, 784, 130, 785, 788, 655, 1283, 388, 396, 1285, 792, 1289, 1298,
-        769, 397, 1302, 770, 1411, 143, 772, 780, 1286, 1413, 1291, 1426, 1299, 781, 1430, 783, 1301, 1931, 1294, 1303,
-        1287, 1280, 1290, 1429, 1296, 1297, 1422, 1300, 1431, 1927, 1304, 1920, 1428, 1292, 1293,
+        773, 10, 135, 777, 786, 16, 790, 17, 774, 779, 20, 24, 641, 789, 384, 138, 144, 642, 145, 148,
+        644, 775, 652, 653, 152, 768, 385, 778, 784, 130, 785, 788, 655, 1283, 388, 1285, 396, 1289, 1298, 397,
+        1302, 769, 792, 770, 1411, 1286, 143, 1413, 772, 780, 1291, 1426, 1299, 781, 1430, 1294, 783, 1931, 1301, 1303,
+        1422, 1287, 1280, 1290, 1296, 1297, 1300, 1429, 1431, 1927, 1920, 1304, 1428, 1292, 1293,
     ),
     (
-        514, 266, 269, 3, 4, 518, 5, 7, 11, 14, 15, 524, 394, 1536, 397, 640, 1664, 1800, 1801, 1811,
-        131, 132, 133, 135, 528, 641, 18, 139, 142, 657, 143, 909, 899, 128, 146, 385, 1032, 1033, 145, 1024,
-        1043, 1034, 1025, 1160, 1028, 1161, 1155, 1029, 1041, 1031, 1165, 1035, 1038, 1152, 1171, 1162, 1153, 1039, 1156, 1026,
-        1157, 1042, 1169, 1030, 1159, 1036, 1040, 1163, 1166, 1167, 1154, 1170, 1158, 1422, 1164, 1168, 1410,
+        514, 266, 269, 3, 4, 518, 5, 7, 11, 14, 15, 524, 1536, 394, 397, 640, 1664, 1800, 1801, 1811,
+        131, 132, 133, 528, 18, 135, 641, 139, 142, 657, 143, 909, 899, 128, 146, 385, 1032, 1033, 145, 1034,
+        1024, 1043, 1025, 1028, 1029, 1160, 1155, 1161, 1031, 1165, 1041, 1035, 1038, 1162, 1152, 1171, 1153, 1156, 1039, 1157,
+        1026, 1042, 1159, 1169, 1030, 1036, 1040, 1163, 1166, 1167, 1154, 1170, 1158, 1164, 1422, 1168, 1410,
     ),
     (
         512, 513, 262, 267, 277, 7, 1536, 648, 1664, 1795, 1797, 1801, 1810, 1814, 390, 395, 514, 405, 516, 654,
-        524, 659, 135, 136, 525, 663, 1027, 527, 10, 16, 403, 17, 1029, 1033, 1042, 1046, 20, 24, 1155, 142,
-        1032, 1030, 138, 1035, 407, 144, 1043, 145, 1157, 148, 1045, 1161, 1170, 1038, 1174, 1160, 1158, 152, 1047, 1163,
-        1031, 1171, 1024, 1173, 1034, 1040, 1166, 1041, 1175, 1044, 1931, 1048, 1159, 1025, 1152, 1026, 1028, 1162, 1036, 1168,
-        1169, 1037, 1172, 1927, 1039, 1920, 1176, 1153, 1154, 1156, 1164, 1165, 1167, 1409, 1410, 1412, 1943,
+        524, 659, 135, 525, 136, 663, 1027, 527, 10, 16, 403, 1029, 17, 20, 1033, 1042, 24, 1046, 1032, 1155,
+        142, 1030, 138, 1035, 407, 144, 1043, 1157, 145, 1161, 148, 1170, 1038, 1174, 1160, 1045, 1158, 1163, 152, 1171,
+        1047, 1031, 1166, 1024, 1034, 1040, 1931, 1173, 1041, 1044, 1175, 1025, 1159, 1152, 1162, 1048, 1168, 1026, 1169, 1028,
+        1172, 1036, 1037, 1927, 1153, 1920, 1039, 1176, 1154, 1156, 1164, 1165, 1167, 1409, 1410, 1412, 1943,
     ),
 )
 

time: 46.6 us -> 46.4 us (level)
  the two profiles are of different devices: /device:TPU:0 before, /device:TPU:1 now
where the time goes in v6:
time: 46.4 us; the launch traced here: 46.3 us
  Pallas kernels  45.7 us (98%)
  between operations  0.64 us (1%)
    pallas_call x1, Pallas kernels, fast(): pl.pallas_call(functools.partial(fused_kernel, depth, factor, inverse), o...  44.6 us
    pallas_call x1, Pallas kernels, fast(): pl.pallas_call(write_out, out_shape=shapes, in_specs=[vmem] * 5, out_spec...  1.05 us

profile of v6, /device:TPU:1, one launch (start us, length us, event | category | flops | bytes accessed | tf_op | source)
XLA Modules:
  0.0 46.3 jit_solution(15938213953319268579)
XLA Ops:
  0.6 44.6 %shard_map.110 = (bf16[128,128]{1,0:T(8,128)(2,1)S(1)}, bf16[128,128]{1,0:T(8,128)(2,1)S(1)}, bf16[128,128]{1,0:T(8,128)(2,1)S(1)}, f32[2048,128]{1,0:T(8,128)S(1)}, f32[96,128]{1,0:T(8,128)S(1)}) custom-call(bf16[128,8192]{1,0:T(8,128)(2,1)} %bitcast.8, bf16[8192,128]{1,0:T(8,128)(2,1)} %w_hbm.1, bf16[384,128]{1,0:T(8,128)(2,1)} %u_hbm.1, ...), custom_call_target="tpu_custom_call" | custom-call | tf_op jit(solution)/shard_map/pallas_call | solution.py:690
  45.2 1.1 %shard_map.111 = (bf16[128,128]{1,0:T(8,128)(2,1)}, bf16[128,128]{1,0:T(8,128)(2,1)}, bf16[128,128]{1,0:T(8,128)(2,1)}, f32[2048,128]{1,0:T(8,128)}, f32[96,128]{1,0:T(8,128)}) custom-call(bf16[128,128]{1,0:T(8,128)(2,1)S(1)} %get-tuple-element.15.refs_0_, bf16[128,128]{1,0:T(8,128)(2,1)S(1)} %get-tuple-element.16.refs_1_, ...), custom_call_target="tpu_custom_call" | custom-call | tf_op jit(solution)/shard_map/pallas_call | solution.py:747
